TPU v7x, 32 devices: a whole 2x2x4 slice. The times are simulated.
32 devices in a mesh: ta: 4 (over x, core), ha: 4 (over z), wa: 2 (over y).
Axes of the slice: x: 2, y: 2, z: 4, core: 2. Of those that a mesh axis runs over, the one named last changes fastest.
Arguments:
- teacher_in: bfloat16 [8, 128, 16, 192], P('ta', 'ha', 'wa'), may hold values from -3 to 3
- teacher_weights: bfloat16 [1, 2, 3, 3, 3, 192, 192], replicated, may hold values from -0.4375 to 0.4375
- student_in: bfloat16 [8, 128, 16, 128], P('ta', ('ha', 'wa')), may hold values from -6 to 6
- depth_weights: float32 [4, 3, 3, 3, 128], replicated, may hold values from -1.25 to 1.25
- point_weights: bfloat16 [4, 128, 128], replicated, may hold values from -0.5 to 0.5
- project_weight: bfloat16 [128, 192], replicated, may hold values from -0.5 to 0.5
Outputs:
- voxel_grad: bfloat16 [8, 128, 16, 128], P('ta', ('ha', 'wa'))
All inputs are finite; a program needn't handle non-finite values.
Results may differ from a plain program's by a relative error of at most 0.01.
Values may be sent and summed in bfloat16 or wider, within the bound.
No kernel may reach another device: no remote copies, remote signals or barrier semaphores. Data moves between devices by JAX's collectives and lax.ppermute only.
A program may use at most 128 MiB of HBM per device.

v0:
```python
import jax
import jax.numpy as jnp
from jax import lax
from jax.sharding import PartitionSpec as P


def from_behind(block, axis, distance):
    devices = range(lax.axis_size(axis))
    route = [(i - distance, i) for i in devices if i - distance in devices]
    return lax.ppermute(block, axis, route)


def extended_2(block, sides, width):
    for axis, dim in sides:
        count = lax.axis_size(axis)
        forward = [(i, i + 1) for i in range(count - 1)]
        backward = [(target, source) for source, target in forward]
        low = lax.ppermute(
            lax.slice_in_dim(block, block.shape[dim] - width, None, axis=dim), axis, forward
        )
        high = lax.ppermute(lax.slice_in_dim(block, 0, width, axis=dim), axis, backward)
        block = jnp.concatenate([low, block, high], axis=dim)
    return block


def root_norm(field):
    return field * lax.rsqrt(jnp.mean(field * field, axis=-1, keepdims=True) + 1e-06)


def silu_slope(field):
    sigmoid_value = jax.nn.sigmoid(field)
    return sigmoid_value * (1.0 + field * (1.0 - sigmoid_value))


def dense_conv(extended, kernel):
    frame_count = extended.shape[0] - 2
    row_count = extended.shape[1] - 2
    col_count = extended.shape[2] - 2
    channels = kernel.shape[-1]
    tap_list = []
    for step_t in range(3):
        for step_h in range(3):
            for step_w in range(3):
                tap_list.append(
                    extended[
                        step_t : step_t + frame_count,
                        step_h : step_h + row_count,
                        step_w : step_w + col_count,
                    ]
                )
    stacked = jnp.concatenate(tap_list, axis=-1).reshape(frame_count * row_count * col_count, -1)
    summed = jnp.dot(stacked, kernel.reshape(-1, channels), preferred_element_type=jnp.float32)
    return summed.reshape(frame_count, row_count, col_count, channels)


def depthwise(extended, kernel):
    frame_count = extended.shape[0] - 2
    row_count = extended.shape[1] - 2
    col_count = extended.shape[2] - 2
    summed = jnp.zeros((frame_count, row_count, col_count, kernel.shape[-1]), jnp.float32)
    for step_t in range(3):
        for step_h in range(3):
            for step_w in range(3):
                tap_slice = extended[
                    step_t : step_t + frame_count,
                    step_h : step_h + row_count,
                    step_w : step_w + col_count,
                ]
                summed = summed + tap_slice.astype(jnp.float32) * kernel[step_t, step_h, step_w]
    return summed


def teacher_extend(active):
    earlier = from_behind(active, "ta", 1)
    longer = jnp.concatenate([earlier, active], axis=0)
    return extended_2(longer, (("ha", 1), ("wa", 2)), 1)


def rows_border(longer):
    widened = extended_2(longer, ((("ha", "wa"), 1),), 1)
    return jnp.pad(widened, ((0, 0), (0, 0), (1, 1), (0, 0)))


def rows_extend_past(active):
    earlier = from_behind(active, "ta", 1)
    return rows_border(jnp.concatenate([earlier, active], axis=0))


def rows_extend_future(backward):
    upcoming = from_behind(backward, "ta", -1)
    return rows_border(jnp.concatenate([backward, upcoming], axis=0))


def student_pass(
    initial, target, depth_weights, point_weights, project_weight, extend_past, extend_future
):
    channels = initial.shape[-1]
    current = initial.astype(jnp.float32)
    stored = []
    for layer_index in range(depth_weights.shape[0]):
        active = jax.nn.silu(current).astype(jnp.bfloat16)
        spread = depthwise(extend_past(active), depth_weights[layer_index]).astype(jnp.bfloat16)
        stored.append(current)
        mixed = jnp.dot(
            spread.reshape(-1, channels),
            point_weights[layer_index],
            preferred_element_type=jnp.float32,
        )
        current = current + mixed.reshape(current.shape)
    projected = jnp.dot(
        current.astype(jnp.bfloat16).reshape(-1, channels),
        project_weight,
        preferred_element_type=jnp.float32,
    )
    mismatch = (projected - target.astype(jnp.float32).reshape(projected.shape)).astype(
        jnp.bfloat16
    )
    gradient = lax.dot_general(
        mismatch, project_weight, (((1,), (1,)), ((), ())), preferred_element_type=jnp.float32
    ).reshape(current.shape)
    for layer_index in reversed(range(depth_weights.shape[0])):
        backward = lax.dot_general(
            gradient.astype(jnp.bfloat16).reshape(-1, channels),
            point_weights[layer_index],
            (((1,), (1,)), ((), ())),
            preferred_element_type=jnp.float32,
        )
        backward = backward.astype(jnp.bfloat16).reshape(current.shape)
        flipped = depth_weights[layer_index][::-1, ::-1, ::-1]
        spread_back = depthwise(extend_future(backward), flipped)
        gradient = gradient + spread_back * silu_slope(stored[layer_index])
    return gradient.astype(jnp.bfloat16)


def on_device(
    teacher_in, teacher_weights, student_in, depth_weights, point_weights, project_weight
):
    target = teacher_in
    current = target.astype(jnp.float32)
    active = jax.nn.silu(root_norm(current)).astype(jnp.bfloat16)
    middle = dense_conv(teacher_extend(active), teacher_weights[0, 0])
    second = jax.nn.silu(root_norm(middle)).astype(jnp.bfloat16)
    target = (current + dense_conv(teacher_extend(second), teacher_weights[0, 1])).astype(
        jnp.bfloat16
    )
    regrouped = lax.all_to_all(target, "wa", split_axis=1, concat_axis=2, tiled=True)
    return student_pass(
        student_in,
        regrouped,
        depth_weights,
        point_weights,
        project_weight,
        rows_extend_past,
        rows_extend_future,
    )


def solution(mesh):
    placed = (P("ta", "ha", "wa", None), P(), P("ta", ("ha", "wa"), None, None), P(), P(), P())
    return jax.shard_map(
        on_device,
        mesh=mesh,
        in_specs=placed,
        out_specs=P("ta", ("ha", "wa"), None, None),
        check_vma=False,
    )
```

profile of v0, /device:TPU:17, one launch (start us, length us, event | category | flops | bytes accessed | tf_op | source)
XLA Modules:
  0.0 208.7 jit_solution(13237344071421855870)
XLA Ops:
  2.3 3.7 %collective-permute-start.12 = (bf16[2,32,8,192]{3,2,1,0:T(8,128)(2,1)S(1)}, bf16[2,32,8,192]{3,2,1,0:T(8,128)(2,1)S(1)}, u32[]{:S(2)}, u32[]{:S(2)}) collective-permute-start(bf16[2,32,8,192]{3,2,1,0:T(8,128)(2,1)S(1)} %fusion.10), channel_id=1, source_target_pairs={{0,8},{8,16},{16,24},{1,9},{9,17},{17,25},{2,10},{10,18},{18,26},{... | collective-permute-start | bytes 589832 | tf_op jit(solution)/shard_map/ppermute | solution.py:10
  11.4 4.7 %fusion.48 = (bf16[1,1,3,3,3,192,192]{6,5,4,3,2,1,0:T(8,128)(2,1)S(1)}, bf16[1,1,3,3,3,192,192]{6,5,4,3,2,1,0:T(8,128)(2,1)}) fusion(bf16[1,2,3,3,3,192,192]{6,5,4,3,2,1,0:T(8,128)(2,1)} %param.7), kind=kLoop, calls=%fused_computation.279 | loop fusion | bytes 7962624 | tf_op jit(solution)/shard_map/slice | solution.py:143
  18.1 3.0 %collective-permute-start.2 = (bf16[4,1,16,128]{3,2,1,0:T(8,128)(2,1)S(1)}, bf16[4,1,16,128]{3,2,1,0:T(8,128)(2,1)S(1)}, u32[]{:S(2)}, u32[]{:S(2)}) collective-permute-start(bf16[4,1,16,128]{3,2,1,0:T(8,128)(2,1)S(1)} %get-tuple-element.108), channel_id=1, source_target_pairs={{1,0},{2,1},{3,2},{4,3},{5,4},{6,5},{7,6},{9,8},{10,9},{11,10},{12... | collective-permute-start | bytes 49160 | tf_op jit(solution)/shard_map/ppermute | solution.py:21
  24.0 2.5 %collective-permute-done.1 = bf16[4,1,16,128]{3,2,1,0:T(8,128)(2,1)S(1)} collective-permute-done((bf16[4,1,16,128]{3,2,1,0:T(8,128)(2,1)S(1)}, bf16[4,1,16,128]{3,2,1,0:T(8,128)(2,1)S(1)}, u32[]{:S(2)}, u32[]{:S(2)}) %collective-permute-start.1) | collective-permute-done | bytes 16416 | tf_op jit(solution)/shard_map/ppermute | solution.py:18
  29.4 3.3 %collective-permute-start.3 = (bf16[2,16,16,128]{3,2,1,0:T(8,128)(2,1)S(1)}, bf16[2,16,16,128]{3,2,1,0:T(8,128)(2,1)S(1)}, u32[]{:S(2)}, u32[]{:S(2)}) collective-permute-start(bf16[2,16,16,128]{3,2,1,0:T(8,128)(2,1)S(1)} %get-tuple-element.223), channel_id=1, source_target_pairs={{0,8},{8,16},{16,24},{1,9},{9,17},{17,25},{2,10},{10,18},{18,26},{... | collective-permute-start | bytes 393224 | tf_op jit(solution)/shard_map/ppermute | solution.py:10
  34.9 3.2 %collective-permute-start.13 = (bf16[4,1,8,192]{3,2,1,0:T(8,128)(2,1)S(1)}, bf16[4,1,8,192]{3,2,1,0:T(8,128)(2,1)S(1)}, u32[]{:S(2)}, u32[]{:S(2)}) collective-permute-start(bf16[4,1,8,192]{3,2,1,0:T(8,128)(2,1)S(1)} %get-tuple-element.75), channel_id=1, source_target_pairs={{0,2},{2,4},{4,6},{1,3},{3,5},{5,7},{8,10},{10,12},{12,14},{9,11},... | collective-permute-start | bytes 36872 | tf_op jit(solution)/shard_map/ppermute | solution.py:18
  40.9 4.0 %collective-permute-start.15 = (bf16[4,34,1,192]{3,2,1,0:T(2,128)(2,1)S(1)}, bf16[4,34,1,192]{3,2,1,0:T(2,128)(2,1)S(1)}, u32[]{:S(2)}, u32[]{:S(2)}) collective-permute-start(bf16[4,34,1,192]{3,2,1,0:T(2,128)(2,1)S(1)} %get-tuple-element.56), channel_id=1, source_target_pairs={{0,1},{2,3},{4,5},{6,7},{8,9},{10,11},{12,13},{14,15},{16,17},{18,... | collective-permute-start | bytes 156680 | tf_op jit(solution)/shard_map/ppermute | solution.py:18
  49.9 10.1 %concatenate.234 = bf16[2,32,8,5184]{3,2,1,0:T(8,128)(2,1)} concatenate(bf16[2,32,8,192]{3,2,1,0:T(8,128)(2,1)} %get-tuple-element.229, bf16[2,32,8,192]{3,2,1,0:T(8,128)(2,1)} %get-tuple-element.238, bf16[2,32,8,192]{3,2,1,0:T(8,128)(2,1)} %get-tuple-element.39, bf16[2,32,8,192]{3,2,1,0:T(8,128)(2,1)} %get-tuple-element.230, ...), dimensions={3} | concatenate | bytes 10616832 | tf_op jit(solution)/shard_map/concatenate | solution.py:51
  60.1 3.5 %collective-permute-start.5 = (bf16[4,1,16,128]{3,2,1,0:T(8,128)(2,1)S(1)}, bf16[4,1,16,128]{3,2,1,0:T(8,128)(2,1)S(1)}, u32[]{:S(2)}, u32[]{:S(2)}) collective-permute-start(bf16[4,1,16,128]{3,2,1,0:T(8,128)(2,1)S(1)} %get-tuple-element.104), channel_id=1, source_target_pairs={{1,0},{2,1},{3,2},{4,3},{5,4},{6,5},{7,6},{9,8},{10,9},{11,10},{12... | collective-permute-start | bytes 49160 | tf_op jit(solution)/shard_map/ppermute | solution.py:21
  65.9 5.1 %multiply_reduce_fusion = (f32[2,32,8]{2,1,0:T(8,128)S(1)}, f32[2,32,8,192]{3,2,1,0:T(8,128)S(1)}) fusion(bf16[2,32,8,5184]{3,2,1,0:T(8,128)(2,1)} %concatenate.234, bf16[5184,192,1,1]{1,0,3,2:T(8,128)(2,1)} %bitcast.317), kind=kOutput, calls=%fused_computation.35 | convolution fusion | flops 1019411968 | bytes 7694336 | tf_op jit(solution)/shard_map/dot_general | solution.py:52
  72.6 5.1 %collective-permute-start.6 = (bf16[2,16,16,128]{3,2,1,0:T(8,128)(2,1)S(1)}, bf16[2,16,16,128]{3,2,1,0:T(8,128)(2,1)S(1)}, u32[]{:S(2)}, u32[]{:S(2)}) collective-permute-start(bf16[2,16,16,128]{3,2,1,0:T(8,128)(2,1)S(1)} %get-tuple-element.225), channel_id=1, source_target_pairs={{0,8},{8,16},{16,24},{1,9},{9,17},{17,25},{2,10},{10,18},{18,26},{... | collective-permute-start | bytes 393224 | tf_op jit(solution)/shard_map/ppermute | solution.py:10
  79.6 4.0 %collective-permute-start.8 = (bf16[4,1,16,128]{3,2,1,0:T(8,128)(2,1)S(1)}, bf16[4,1,16,128]{3,2,1,0:T(8,128)(2,1)S(1)}, u32[]{:S(2)}, u32[]{:S(2)}) collective-permute-start(bf16[4,1,16,128]{3,2,1,0:T(8,128)(2,1)S(1)} %get-tuple-element.100), channel_id=1, source_target_pairs={{1,0},{2,1},{3,2},{4,3},{5,4},{6,5},{7,6},{9,8},{10,9},{11,10},{12... | collective-permute-start | bytes 49160 | tf_op jit(solution)/shard_map/ppermute | solution.py:21
  83.6 2.5 %collective-permute-start.7 = (bf16[4,1,16,128]{3,2,1,0:T(8,128)(2,1)S(1)}, bf16[4,1,16,128]{3,2,1,0:T(8,128)(2,1)S(1)}, u32[]{:S(2)}, u32[]{:S(2)}) collective-permute-start(bf16[4,1,16,128]{3,2,1,0:T(8,128)(2,1)S(1)} %get-tuple-element.99), channel_id=1, source_target_pairs={{0,1},{1,2},{2,3},{3,4},{4,5},{5,6},{6,7},{8,9},{9,10},{10,11},{11... | collective-permute-start | bytes 49160 | tf_op jit(solution)/shard_map/ppermute | solution.py:18
  86.3 4.6 %collective-permute-start.17 = (bf16[2,32,8,192]{3,2,1,0:T(8,128)(2,1)S(1)}, bf16[2,32,8,192]{3,2,1,0:T(8,128)(2,1)S(1)}, u32[]{:S(2)}, u32[]{:S(2)}) collective-permute-start(bf16[2,32,8,192]{3,2,1,0:T(8,128)(2,1)S(1)} %multiply_convert_fusion), channel_id=1, source_target_pairs={{0,8},{8,16},{16,24},{1,9},{9,17},{17,25},{2,10},{10,18},{18,26},{... | collective-permute-start | bytes 589832 | tf_op jit(solution)/shard_map/ppermute | solution.py:10
  93.1 3.8 %collective-permute-start.9 = (bf16[2,16,16,128]{3,2,1,0:T(8,128)(2,1)S(1)}, bf16[2,16,16,128]{3,2,1,0:T(8,128)(2,1)S(1)}, u32[]{:S(2)}, u32[]{:S(2)}) collective-permute-start(bf16[2,16,16,128]{3,2,1,0:T(8,128)(2,1)S(1)} %get-tuple-element.227), channel_id=1, source_target_pairs={{0,8},{8,16},{16,24},{1,9},{9,17},{17,25},{2,10},{10,18},{18,26},{... | collective-permute-start | bytes 393224 | tf_op jit(solution)/shard_map/ppermute | solution.py:10
  98.8 3.4 %collective-permute-start.18 = (bf16[4,1,8,192]{3,2,1,0:T(8,128)(2,1)S(1)}, bf16[4,1,8,192]{3,2,1,0:T(8,128)(2,1)S(1)}, u32[]{:S(2)}, u32[]{:S(2)}) collective-permute-start(bf16[4,1,8,192]{3,2,1,0:T(8,128)(2,1)S(1)} %get-tuple-element.71), channel_id=1, source_target_pairs={{0,2},{2,4},{4,6},{1,3},{3,5},{5,7},{8,10},{10,12},{12,14},{9,11},... | collective-permute-start | bytes 36872 | tf_op jit(solution)/shard_map/ppermute | solution.py:18
  104.8 4.2 %collective-permute-start.20 = (bf16[4,34,1,192]{3,2,1,0:T(2,128)(2,1)S(1)}, bf16[4,34,1,192]{3,2,1,0:T(2,128)(2,1)S(1)}, u32[]{:S(2)}, u32[]{:S(2)}) collective-permute-start(bf16[4,34,1,192]{3,2,1,0:T(2,128)(2,1)S(1)} %get-tuple-element.52), channel_id=1, source_target_pairs={{0,1},{2,3},{4,5},{6,7},{8,9},{10,11},{12,13},{14,15},{16,17},{18,... | collective-permute-start | bytes 156680 | tf_op jit(solution)/shard_map/ppermute | solution.py:18
  115.3 10.1 %concatenate.241 = bf16[2,32,8,5184]{3,2,1,0:T(8,128)(2,1)} concatenate(bf16[2,32,8,192]{3,2,1,0:T(8,128)(2,1)} %get-tuple-element.30, bf16[2,32,8,192]{3,2,1,0:T(8,128)(2,1)} %get-tuple-element.62, bf16[2,32,8,192]{3,2,1,0:T(8,128)(2,1)} %get-tuple-element.21, bf16[2,32,8,192]{3,2,1,0:T(8,128)(2,1)} %get-tuple-element.29, bf16[2,32,8,192]{3,2,1,0:T(8,128)(2,1)S(1)} %collective-permute-done.17, ...), dimensions={3} | concatenate | bytes 10616832 | tf_op jit(solution)/shard_map/concatenate | solution.py:51
  125.5 3.6 %collective-permute-start.11 = (bf16[4,1,16,128]{3,2,1,0:T(8,128)(2,1)S(1)}, bf16[4,1,16,128]{3,2,1,0:T(8,128)(2,1)S(1)}, u32[]{:S(2)}, u32[]{:S(2)}) collective-permute-start(bf16[4,1,16,128]{3,2,1,0:T(8,128)(2,1)S(1)} %get-tuple-element.96), channel_id=1, source_target_pairs={{1,0},{2,1},{3,2},{4,3},{5,4},{6,5},{7,6},{9,8},{10,9},{11,10},{12... | collective-permute-start | bytes 49160 | tf_op jit(solution)/shard_map/ppermute | solution.py:21
  129.0 2.4 %collective-permute-start.10 = (bf16[4,1,16,128]{3,2,1,0:T(8,128)(2,1)S(1)}, bf16[4,1,16,128]{3,2,1,0:T(8,128)(2,1)S(1)}, u32[]{:S(2)}, u32[]{:S(2)}) collective-permute-start(bf16[4,1,16,128]{3,2,1,0:T(8,128)(2,1)S(1)} %get-tuple-element.95), channel_id=1, source_target_pairs={{0,1},{1,2},{2,3},{3,4},{4,5},{5,6},{6,7},{8,9},{9,10},{10,11},{11... | collective-permute-start | bytes 49160 | tf_op jit(solution)/shard_map/ppermute | solution.py:18
  131.5 4.1 %fusion = bf16[2,32,8,192]{3,2,1,0:T(8,128)(2,1)S(1)} fusion(bf16[2,32,8,5184]{3,2,1,0:T(8,128)(2,1)} %concatenate.241, bf16[5184,192,1,1]{1,0,3,2:T(8,128)(2,1)S(1)} %bitcast.316, bf16[2,32,8,192]{3,2,1,0:T(8,128)(2,1)} %param.6), kind=kOutput, calls=%fused_computation.4 | convolution fusion | flops 1019510784 | bytes 7692288 | tf_op jit(solution)/shard_map/dot_general | solution.py:52
  136.6 3.6 %all-to-all-start = ((bf16[2,32,8,192]{3,2,0,1:T(8,128)(2,1)}), bf16[2,32,8,192]{3,2,0,1:T(8,128)(2,1)S(1)}, u32[]{:S(2)}, u32[]{:S(2)}) async-start(bf16[2,32,8,192]{3,2,0,1:T(8,128)(2,1)} %copy.14), calls=%async_computation | async-start | bytes 524288 | tf_op jit(solution)/shard_map/all_to_all | solution.py:146
  141.7 3.3 %all-to-all-done = bf16[2,32,8,192]{3,2,0,1:T(8,128)(2,1)S(1)} async-done(((bf16[2,32,8,192]{3,2,0,1:T(8,128)(2,1)}), bf16[2,32,8,192]{3,2,0,1:T(8,128)(2,1)S(1)}, u32[]{:S(2)}, u32[]{:S(2)}) %all-to-all-start) | async-done | bytes 196640 | tf_op jit(solution)/shard_map/all_to_all | solution.py:146
  145.9 4.5 %collective-permute-start.22 = (bf16[2,16,16,128]{3,2,1,0:T(8,128)(2,1)S(1)}, bf16[2,16,16,128]{3,2,1,0:T(8,128)(2,1)S(1)}, u32[]{:S(2)}, u32[]{:S(2)}) collective-permute-start(bf16[2,16,16,128]{3,2,1,0:T(8,128)(2,1)S(1)} %bitcast.306), channel_id=1, source_target_pairs={{8,0},{16,8},{24,16},{9,1},{17,9},{25,17},{10,2},{18,10},{26,18},{... | collective-permute-start | bytes 393224 | tf_op jit(solution)/shard_map/ppermute | solution.py:10
  150.4 3.1 %collective-permute-done.22 = bf16[2,16,16,128]{3,2,1,0:T(8,128)(2,1)S(1)} collective-permute-done((bf16[2,16,16,128]{3,2,1,0:T(8,128)(2,1)S(1)}, bf16[2,16,16,128]{3,2,1,0:T(8,128)(2,1)S(1)}, u32[]{:S(2)}, u32[]{:S(2)}) %collective-permute-start.22) | collective-permute-done | bytes 131104 | tf_op jit(solution)/shard_map/ppermute | solution.py:10
  155.5 3.4 %collective-permute-start.23 = (bf16[4,1,16,128]{3,2,1,0:T(8,128)(2,1)S(1)}, bf16[4,1,16,128]{3,2,1,0:T(8,128)(2,1)S(1)}, u32[]{:S(2)}, u32[]{:S(2)}) collective-permute-start(bf16[4,1,16,128]{3,2,1,0:T(8,128)(2,1)S(1)} %get-tuple-element.91), channel_id=1, source_target_pairs={{0,1},{1,2},{2,3},{3,4},{4,5},{5,6},{6,7},{8,9},{9,10},{10,11},{11... | collective-permute-start | bytes 49160 | tf_op jit(solution)/shard_map/ppermute | solution.py:18
  164.3 4.4 %collective-permute-done.25 = bf16[2,16,16,128]{3,2,1,0:T(8,128)(2,1)S(1)} collective-permute-done((bf16[2,16,16,128]{3,2,1,0:T(8,128)(2,1)S(1)}, bf16[2,16,16,128]{3,2,1,0:T(8,128)(2,1)S(1)}, u32[]{:S(2)}, u32[]{:S(2)}) %collective-permute-start.25) | collective-permute-done | bytes 131104 | tf_op jit(solution)/shard_map/ppermute | solution.py:10
  170.6 3.4 %collective-permute-start.26 = (bf16[4,1,16,128]{3,2,1,0:T(8,128)(2,1)S(1)}, bf16[4,1,16,128]{3,2,1,0:T(8,128)(2,1)S(1)}, u32[]{:S(2)}, u32[]{:S(2)}) collective-permute-start(bf16[4,1,16,128]{3,2,1,0:T(8,128)(2,1)S(1)} %get-tuple-element.87), channel_id=1, source_target_pairs={{0,1},{1,2},{2,3},{3,4},{4,5},{5,6},{6,7},{8,9},{9,10},{10,11},{11... | collective-permute-start | bytes 49160 | tf_op jit(solution)/shard_map/ppermute | solution.py:18
  179.6 4.4 %collective-permute-done.28 = bf16[2,16,16,128]{3,2,1,0:T(8,128)(2,1)S(1)} collective-permute-done((bf16[2,16,16,128]{3,2,1,0:T(8,128)(2,1)S(1)}, bf16[2,16,16,128]{3,2,1,0:T(8,128)(2,1)S(1)}, u32[]{:S(2)}, u32[]{:S(2)}) %collective-permute-start.28) | collective-permute-done | bytes 131104 | tf_op jit(solution)/shard_map/ppermute | solution.py:10
  185.9 3.4 %collective-permute-start.29 = (bf16[4,1,16,128]{3,2,1,0:T(8,128)(2,1)S(1)}, bf16[4,1,16,128]{3,2,1,0:T(8,128)(2,1)S(1)}, u32[]{:S(2)}, u32[]{:S(2)}) collective-permute-start(bf16[4,1,16,128]{3,2,1,0:T(8,128)(2,1)S(1)} %get-tuple-element.83), channel_id=1, source_target_pairs={{0,1},{1,2},{2,3},{3,4},{4,5},{5,6},{6,7},{8,9},{9,10},{10,11},{11... | collective-permute-start | bytes 49160 | tf_op jit(solution)/shard_map/ppermute | solution.py:18
  194.9 4.4 %collective-permute-done.31 = bf16[2,16,16,128]{3,2,1,0:T(8,128)(2,1)S(1)} collective-permute-done((bf16[2,16,16,128]{3,2,1,0:T(8,128)(2,1)S(1)}, bf16[2,16,16,128]{3,2,1,0:T(8,128)(2,1)S(1)}, u32[]{:S(2)}, u32[]{:S(2)}) %collective-permute-start.31) | collective-permute-done | bytes 131104 | tf_op jit(solution)/shard_map/ppermute | solution.py:10
  201.2 3.4 %collective-permute-start.32 = (bf16[4,1,16,128]{3,2,1,0:T(8,128)(2,1)S(1)}, bf16[4,1,16,128]{3,2,1,0:T(8,128)(2,1)S(1)}, u32[]{:S(2)}, u32[]{:S(2)}) collective-permute-start(bf16[4,1,16,128]{3,2,1,0:T(8,128)(2,1)S(1)} %get-tuple-element.79), channel_id=1, source_target_pairs={{0,1},{1,2},{2,3},{3,4},{4,5},{5,6},{6,7},{8,9},{9,10},{10,11},{11... | collective-permute-start | bytes 49160 | tf_op jit(solution)/shard_map/ppermute | solution.py:18
  (450 shorter events, 73.4 us)
Async XLA Ops:
  2.3 30.5 %collective-permute-start.12 = (bf16[2,32,8,192]{3,2,1,0:T(8,128)(2,1)S(1)}, bf16[2,32,8,192]{3,2,1,0:T(8,128)(2,1)S(1)}, u32[]{:S(2)}, u32[]{:S(2)}) collective-permute-start(bf16[2,32,8,192]{3,2,1,0:T(8,128)(2,1)S(1)} %fusion.10), channel_id=1, source_target_pairs={{0,8},{8,16},{16,24},{1,9},{9,17},{17,25},{2,10},{10,18},{18,26},{... | collective-permute-start | bytes 589832 | tf_op jit(solution)/shard_map/ppermute | solution.py:10
  7.0 11.1 %collective-permute-start = (bf16[2,16,16,128]{3,2,1,0:T(8,128)(2,1)S(1)}, bf16[2,16,16,128]{3,2,1,0:T(8,128)(2,1)S(1)}, u32[]{:S(2)}, u32[]{:S(2)}) collective-permute-start(bf16[2,16,16,128]{3,2,1,0:T(8,128)(2,1)S(1)} %fusion.18), channel_id=1, source_target_pairs={{0,8},{8,16},{16,24},{1,9},{9,17},{17,25},{2,10},{10,18},{18,26},{... | collective-permute-start | bytes 393224 | tf_op jit(solution)/shard_map/ppermute | solution.py:10
  18.1 5.9 %collective-permute-start.2 = (bf16[4,1,16,128]{3,2,1,0:T(8,128)(2,1)S(1)}, bf16[4,1,16,128]{3,2,1,0:T(8,128)(2,1)S(1)}, u32[]{:S(2)}, u32[]{:S(2)}) collective-permute-start(bf16[4,1,16,128]{3,2,1,0:T(8,128)(2,1)S(1)} %get-tuple-element.108), channel_id=1, source_target_pairs={{1,0},{2,1},{3,2},{4,3},{5,4},{6,5},{7,6},{9,8},{10,9},{11,10},{12... | collective-permute-start | bytes 49160 | tf_op jit(solution)/shard_map/ppermute | solution.py:21
  21.1 5.4 %collective-permute-start.1 = (bf16[4,1,16,128]{3,2,1,0:T(8,128)(2,1)S(1)}, bf16[4,1,16,128]{3,2,1,0:T(8,128)(2,1)S(1)}, u32[]{:S(2)}, u32[]{:S(2)}) collective-permute-start(bf16[4,1,16,128]{3,2,1,0:T(8,128)(2,1)S(1)} %get-tuple-element.107), channel_id=1, source_target_pairs={{0,1},{1,2},{2,3},{3,4},{4,5},{5,6},{6,7},{8,9},{9,10},{10,11},{11... | collective-permute-start | bytes 49160 | tf_op jit(solution)/shard_map/ppermute | solution.py:18
  29.4 30.6 %collective-permute-start.3 = (bf16[2,16,16,128]{3,2,1,0:T(8,128)(2,1)S(1)}, bf16[2,16,16,128]{3,2,1,0:T(8,128)(2,1)S(1)}, u32[]{:S(2)}, u32[]{:S(2)}) collective-permute-start(bf16[2,16,16,128]{3,2,1,0:T(8,128)(2,1)S(1)} %get-tuple-element.223), channel_id=1, source_target_pairs={{0,8},{8,16},{16,24},{1,9},{9,17},{17,25},{2,10},{10,18},{18,26},{... | collective-permute-start | bytes 393224 | tf_op jit(solution)/shard_map/ppermute | solution.py:10
  32.8 6.1 %collective-permute-start.14 = (bf16[4,1,8,192]{3,2,1,0:T(8,128)(2,1)S(1)}, bf16[4,1,8,192]{3,2,1,0:T(8,128)(2,1)S(1)}, u32[]{:S(2)}, u32[]{:S(2)}) collective-permute-start(bf16[4,1,8,192]{3,2,1,0:T(8,128)(2,1)S(1)} %get-tuple-element.76), channel_id=1, source_target_pairs={{2,0},{4,2},{6,4},{3,1},{5,3},{7,5},{10,8},{12,10},{14,12},{11,9},... | collective-permute-start | bytes 36872 | tf_op jit(solution)/shard_map/ppermute | solution.py:21
  39.6 6.7 %collective-permute-start.16 = (bf16[4,34,1,192]{3,2,1,0:T(2,128)(2,1)S(1)}, bf16[4,34,1,192]{3,2,1,0:T(2,128)(2,1)S(1)}, u32[]{:S(2)}, u32[]{:S(2)}) collective-permute-start(bf16[4,34,1,192]{3,2,1,0:T(2,128)(2,1)S(1)} %get-tuple-element.55), channel_id=1, source_target_pairs={{1,0},{3,2},{5,4},{7,6},{9,8},{11,10},{13,12},{15,14},{17,16},{19,... | collective-permute-start | bytes 156680 | tf_op jit(solution)/shard_map/ppermute | solution.py:21
  40.9 6.0 %collective-permute-start.15 = (bf16[4,34,1,192]{3,2,1,0:T(2,128)(2,1)S(1)}, bf16[4,34,1,192]{3,2,1,0:T(2,128)(2,1)S(1)}, u32[]{:S(2)}, u32[]{:S(2)}) collective-permute-start(bf16[4,34,1,192]{3,2,1,0:T(2,128)(2,1)S(1)} %get-tuple-element.56), channel_id=1, source_target_pairs={{0,1},{2,3},{4,5},{6,7},{8,9},{10,11},{12,13},{14,15},{16,17},{18,... | collective-permute-start | bytes 156680 | tf_op jit(solution)/shard_map/ppermute | solution.py:18
  60.1 10.9 %collective-permute-start.5 = (bf16[4,1,16,128]{3,2,1,0:T(8,128)(2,1)S(1)}, bf16[4,1,16,128]{3,2,1,0:T(8,128)(2,1)S(1)}, u32[]{:S(2)}, u32[]{:S(2)}) collective-permute-start(bf16[4,1,16,128]{3,2,1,0:T(8,128)(2,1)S(1)} %get-tuple-element.104), channel_id=1, source_target_pairs={{1,0},{2,1},{3,2},{4,3},{5,4},{6,5},{7,6},{9,8},{10,9},{11,10},{12... | collective-permute-start | bytes 49160 | tf_op jit(solution)/shard_map/ppermute | solution.py:21
  63.6 7.4 %collective-permute-start.4 = (bf16[4,1,16,128]{3,2,1,0:T(8,128)(2,1)S(1)}, bf16[4,1,16,128]{3,2,1,0:T(8,128)(2,1)S(1)}, u32[]{:S(2)}, u32[]{:S(2)}) collective-permute-start(bf16[4,1,16,128]{3,2,1,0:T(8,128)(2,1)S(1)} %get-tuple-element.103), channel_id=1, source_target_pairs={{0,1},{1,2},{2,3},{3,4},{4,5},{5,6},{6,7},{8,9},{9,10},{10,11},{11... | collective-permute-start | bytes 49160 | tf_op jit(solution)/shard_map/ppermute | solution.py:18
  72.6 7.0 %collective-permute-start.6 = (bf16[2,16,16,128]{3,2,1,0:T(8,128)(2,1)S(1)}, bf16[2,16,16,128]{3,2,1,0:T(8,128)(2,1)S(1)}, u32[]{:S(2)}, u32[]{:S(2)}) collective-permute-start(bf16[2,16,16,128]{3,2,1,0:T(8,128)(2,1)S(1)} %get-tuple-element.225), channel_id=1, source_target_pairs={{0,8},{8,16},{16,24},{1,9},{9,17},{17,25},{2,10},{10,18},{18,26},{... | collective-permute-start | bytes 393224 | tf_op jit(solution)/shard_map/ppermute | solution.py:10
  79.6 11.3 %collective-permute-start.8 = (bf16[4,1,16,128]{3,2,1,0:T(8,128)(2,1)S(1)}, bf16[4,1,16,128]{3,2,1,0:T(8,128)(2,1)S(1)}, u32[]{:S(2)}, u32[]{:S(2)}) collective-permute-start(bf16[4,1,16,128]{3,2,1,0:T(8,128)(2,1)S(1)} %get-tuple-element.100), channel_id=1, source_target_pairs={{1,0},{2,1},{3,2},{4,3},{5,4},{6,5},{7,6},{9,8},{10,9},{11,10},{12... | collective-permute-start | bytes 49160 | tf_op jit(solution)/shard_map/ppermute | solution.py:21
  83.6 7.4 %collective-permute-start.7 = (bf16[4,1,16,128]{3,2,1,0:T(8,128)(2,1)S(1)}, bf16[4,1,16,128]{3,2,1,0:T(8,128)(2,1)S(1)}, u32[]{:S(2)}, u32[]{:S(2)}) collective-permute-start(bf16[4,1,16,128]{3,2,1,0:T(8,128)(2,1)S(1)} %get-tuple-element.99), channel_id=1, source_target_pairs={{0,1},{1,2},{2,3},{3,4},{4,5},{5,6},{6,7},{8,9},{9,10},{10,11},{11... | collective-permute-start | bytes 49160 | tf_op jit(solution)/shard_map/ppermute | solution.py:18
  86.3 10.6 %collective-permute-start.17 = (bf16[2,32,8,192]{3,2,1,0:T(8,128)(2,1)S(1)}, bf16[2,32,8,192]{3,2,1,0:T(8,128)(2,1)S(1)}, u32[]{:S(2)}, u32[]{:S(2)}) collective-permute-start(bf16[2,32,8,192]{3,2,1,0:T(8,128)(2,1)S(1)} %multiply_convert_fusion), channel_id=1, source_target_pairs={{0,8},{8,16},{16,24},{1,9},{9,17},{17,25},{2,10},{10,18},{18,26},{... | collective-permute-start | bytes 589832 | tf_op jit(solution)/shard_map/ppermute | solution.py:10
  93.1 32.3 %collective-permute-start.9 = (bf16[2,16,16,128]{3,2,1,0:T(8,128)(2,1)S(1)}, bf16[2,16,16,128]{3,2,1,0:T(8,128)(2,1)S(1)}, u32[]{:S(2)}, u32[]{:S(2)}) collective-permute-start(bf16[2,16,16,128]{3,2,1,0:T(8,128)(2,1)S(1)} %get-tuple-element.227), channel_id=1, source_target_pairs={{0,8},{8,16},{16,24},{1,9},{9,17},{17,25},{2,10},{10,18},{18,26},{... | collective-permute-start | bytes 393224 | tf_op jit(solution)/shard_map/ppermute | solution.py:10
  96.9 6.1 %collective-permute-start.19 = (bf16[4,1,8,192]{3,2,1,0:T(8,128)(2,1)S(1)}, bf16[4,1,8,192]{3,2,1,0:T(8,128)(2,1)S(1)}, u32[]{:S(2)}, u32[]{:S(2)}) collective-permute-start(bf16[4,1,8,192]{3,2,1,0:T(8,128)(2,1)S(1)} %get-tuple-element.72), channel_id=1, source_target_pairs={{2,0},{4,2},{6,4},{3,1},{5,3},{7,5},{10,8},{12,10},{14,12},{11,9},... | collective-permute-start | bytes 36872 | tf_op jit(solution)/shard_map/ppermute | solution.py:21
  103.5 7.6 %collective-permute-start.21 = (bf16[4,34,1,192]{3,2,1,0:T(2,128)(2,1)S(1)}, bf16[4,34,1,192]{3,2,1,0:T(2,128)(2,1)S(1)}, u32[]{:S(2)}, u32[]{:S(2)}) collective-permute-start(bf16[4,34,1,192]{3,2,1,0:T(2,128)(2,1)S(1)} %get-tuple-element.51), channel_id=1, source_target_pairs={{1,0},{3,2},{5,4},{7,6},{9,8},{11,10},{13,12},{15,14},{17,16},{19,... | collective-permute-start | bytes 156680 | tf_op jit(solution)/shard_map/ppermute | solution.py:21
  104.8 6.7 %collective-permute-start.20 = (bf16[4,34,1,192]{3,2,1,0:T(2,128)(2,1)S(1)}, bf16[4,34,1,192]{3,2,1,0:T(2,128)(2,1)S(1)}, u32[]{:S(2)}, u32[]{:S(2)}) collective-permute-start(bf16[4,34,1,192]{3,2,1,0:T(2,128)(2,1)S(1)} %get-tuple-element.52), channel_id=1, source_target_pairs={{0,1},{2,3},{4,5},{6,7},{8,9},{10,11},{12,13},{14,15},{16,17},{18,... | collective-permute-start | bytes 156680 | tf_op jit(solution)/shard_map/ppermute | solution.py:18
  125.5 14.8 %collective-permute-start.11 = (bf16[4,1,16,128]{3,2,1,0:T(8,128)(2,1)S(1)}, bf16[4,1,16,128]{3,2,1,0:T(8,128)(2,1)S(1)}, u32[]{:S(2)}, u32[]{:S(2)}) collective-permute-start(bf16[4,1,16,128]{3,2,1,0:T(8,128)(2,1)S(1)} %get-tuple-element.96), channel_id=1, source_target_pairs={{1,0},{2,1},{3,2},{4,3},{5,4},{6,5},{7,6},{9,8},{10,9},{11,10},{12... | collective-permute-start | bytes 49160 | tf_op jit(solution)/shard_map/ppermute | solution.py:21
  129.0 11.2 %collective-permute-start.10 = (bf16[4,1,16,128]{3,2,1,0:T(8,128)(2,1)S(1)}, bf16[4,1,16,128]{3,2,1,0:T(8,128)(2,1)S(1)}, u32[]{:S(2)}, u32[]{:S(2)}) collective-permute-start(bf16[4,1,16,128]{3,2,1,0:T(8,128)(2,1)S(1)} %get-tuple-element.95), channel_id=1, source_target_pairs={{0,1},{1,2},{2,3},{3,4},{4,5},{5,6},{6,7},{8,9},{9,10},{10,11},{11... | collective-permute-start | bytes 49160 | tf_op jit(solution)/shard_map/ppermute | solution.py:18
  136.6 8.3 %all-to-all-start = ((bf16[2,32,8,192]{3,2,0,1:T(8,128)(2,1)}), bf16[2,32,8,192]{3,2,0,1:T(8,128)(2,1)S(1)}, u32[]{:S(2)}, u32[]{:S(2)}) async-start(bf16[2,32,8,192]{3,2,0,1:T(8,128)(2,1)} %copy.14), calls=%async_computation | async-start | bytes 524288 | tf_op jit(solution)/shard_map/all_to_all | solution.py:146
  145.9 7.6 %collective-permute-start.22 = (bf16[2,16,16,128]{3,2,1,0:T(8,128)(2,1)S(1)}, bf16[2,16,16,128]{3,2,1,0:T(8,128)(2,1)S(1)}, u32[]{:S(2)}, u32[]{:S(2)}) collective-permute-start(bf16[2,16,16,128]{3,2,1,0:T(8,128)(2,1)S(1)} %bitcast.306), channel_id=1, source_target_pairs={{8,0},{16,8},{24,16},{9,1},{17,9},{25,17},{10,2},{18,10},{26,18},{... | collective-permute-start | bytes 393224 | tf_op jit(solution)/shard_map/ppermute | solution.py:10
  153.6 5.3 %collective-permute-start.24 = (bf16[4,1,16,128]{3,2,1,0:T(8,128)(2,1)S(1)}, bf16[4,1,16,128]{3,2,1,0:T(8,128)(2,1)S(1)}, u32[]{:S(2)}, u32[]{:S(2)}) collective-permute-start(bf16[4,1,16,128]{3,2,1,0:T(8,128)(2,1)S(1)} %get-tuple-element.92), channel_id=1, source_target_pairs={{1,0},{2,1},{3,2},{4,3},{5,4},{6,5},{7,6},{9,8},{10,9},{11,10},{12... | collective-permute-start | bytes 49160 | tf_op jit(solution)/shard_map/ppermute | solution.py:21
  155.5 5.4 %collective-permute-start.23 = (bf16[4,1,16,128]{3,2,1,0:T(8,128)(2,1)S(1)}, bf16[4,1,16,128]{3,2,1,0:T(8,128)(2,1)S(1)}, u32[]{:S(2)}, u32[]{:S(2)}) collective-permute-start(bf16[4,1,16,128]{3,2,1,0:T(8,128)(2,1)S(1)} %get-tuple-element.91), channel_id=1, source_target_pairs={{0,1},{1,2},{2,3},{3,4},{4,5},{5,6},{6,7},{8,9},{9,10},{10,11},{11... | collective-permute-start | bytes 49160 | tf_op jit(solution)/shard_map/ppermute | solution.py:18
  162.4 6.3 %collective-permute-start.25 = (bf16[2,16,16,128]{3,2,1,0:T(8,128)(2,1)S(1)}, bf16[2,16,16,128]{3,2,1,0:T(8,128)(2,1)S(1)}, u32[]{:S(2)}, u32[]{:S(2)}) collective-permute-start(bf16[2,16,16,128]{3,2,1,0:T(8,128)(2,1)S(1)} %bitcast.296), channel_id=1, source_target_pairs={{8,0},{16,8},{24,16},{9,1},{17,9},{25,17},{10,2},{18,10},{26,18},{... | collective-permute-start | bytes 393224 | tf_op jit(solution)/shard_map/ppermute | solution.py:10
  170.6 5.4 %collective-permute-start.26 = (bf16[4,1,16,128]{3,2,1,0:T(8,128)(2,1)S(1)}, bf16[4,1,16,128]{3,2,1,0:T(8,128)(2,1)S(1)}, u32[]{:S(2)}, u32[]{:S(2)}) collective-permute-start(bf16[4,1,16,128]{3,2,1,0:T(8,128)(2,1)S(1)} %get-tuple-element.87), channel_id=1, source_target_pairs={{0,1},{1,2},{2,3},{3,4},{4,5},{5,6},{6,7},{8,9},{9,10},{10,11},{11... | collective-permute-start | bytes 49160 | tf_op jit(solution)/shard_map/ppermute | solution.py:18
  177.7 6.3 %collective-permute-start.28 = (bf16[2,16,16,128]{3,2,1,0:T(8,128)(2,1)S(1)}, bf16[2,16,16,128]{3,2,1,0:T(8,128)(2,1)S(1)}, u32[]{:S(2)}, u32[]{:S(2)}) collective-permute-start(bf16[2,16,16,128]{3,2,1,0:T(8,128)(2,1)S(1)} %bitcast.301), channel_id=1, source_target_pairs={{8,0},{16,8},{24,16},{9,1},{17,9},{25,17},{10,2},{18,10},{26,18},{... | collective-permute-start | bytes 393224 | tf_op jit(solution)/shard_map/ppermute | solution.py:10
  184.0 5.3 %collective-permute-start.30 = (bf16[4,1,16,128]{3,2,1,0:T(8,128)(2,1)S(1)}, bf16[4,1,16,128]{3,2,1,0:T(8,128)(2,1)S(1)}, u32[]{:S(2)}, u32[]{:S(2)}) collective-permute-start(bf16[4,1,16,128]{3,2,1,0:T(8,128)(2,1)S(1)} %get-tuple-element.84), channel_id=1, source_target_pairs={{1,0},{2,1},{3,2},{4,3},{5,4},{6,5},{7,6},{9,8},{10,9},{11,10},{12... | collective-permute-start | bytes 49160 | tf_op jit(solution)/shard_map/ppermute | solution.py:21
  185.9 5.4 %collective-permute-start.29 = (bf16[4,1,16,128]{3,2,1,0:T(8,128)(2,1)S(1)}, bf16[4,1,16,128]{3,2,1,0:T(8,128)(2,1)S(1)}, u32[]{:S(2)}, u32[]{:S(2)}) collective-permute-start(bf16[4,1,16,128]{3,2,1,0:T(8,128)(2,1)S(1)} %get-tuple-element.83), channel_id=1, source_target_pairs={{0,1},{1,2},{2,3},{3,4},{4,5},{5,6},{6,7},{8,9},{9,10},{10,11},{11... | collective-permute-start | bytes 49160 | tf_op jit(solution)/shard_map/ppermute | solution.py:18
  193.0 6.3 %collective-permute-start.31 = (bf16[2,16,16,128]{3,2,1,0:T(8,128)(2,1)S(1)}, bf16[2,16,16,128]{3,2,1,0:T(8,128)(2,1)S(1)}, u32[]{:S(2)}, u32[]{:S(2)}) collective-permute-start(bf16[2,16,16,128]{3,2,1,0:T(8,128)(2,1)S(1)} %bitcast.311), channel_id=1, source_target_pairs={{8,0},{16,8},{24,16},{9,1},{17,9},{25,17},{10,2},{18,10},{26,18},{... | collective-permute-start | bytes 393224 | tf_op jit(solution)/shard_map/ppermute | solution.py:10
  199.3 5.3 %collective-permute-start.33 = (bf16[4,1,16,128]{3,2,1,0:T(8,128)(2,1)S(1)}, bf16[4,1,16,128]{3,2,1,0:T(8,128)(2,1)S(1)}, u32[]{:S(2)}, u32[]{:S(2)}) collective-permute-start(bf16[4,1,16,128]{3,2,1,0:T(8,128)(2,1)S(1)} %get-tuple-element.80), channel_id=1, source_target_pairs={{1,0},{2,1},{3,2},{4,3},{5,4},{6,5},{7,6},{9,8},{10,9},{11,10},{12... | collective-permute-start | bytes 49160 | tf_op jit(solution)/shard_map/ppermute | solution.py:21
  201.2 5.4 %collective-permute-start.32 = (bf16[4,1,16,128]{3,2,1,0:T(8,128)(2,1)S(1)}, bf16[4,1,16,128]{3,2,1,0:T(8,128)(2,1)S(1)}, u32[]{:S(2)}, u32[]{:S(2)}) collective-permute-start(bf16[4,1,16,128]{3,2,1,0:T(8,128)(2,1)S(1)} %get-tuple-element.79), channel_id=1, source_target_pairs={{0,1},{1,2},{2,3},{3,4},{4,5},{5,6},{6,7},{8,9},{9,10},{10,11},{11... | collective-permute-start | bytes 49160 | tf_op jit(solution)/shard_map/ppermute | solution.py:18
  (170 other events, 2401.8 us)
where the time goes:
time: 212 us; the launch traced here: 209 us
  starting transfers between devices  102 us (48%)
  local copies, waits for them, and re-layouts  39.7 us (19%)
  waiting for transfers between devices  33.8 us (16%)
  matrix products  16.1 us (8%)
  other arithmetic  13.6 us (6%)
  between operations  3.33 us (2%)
    ppermute x12, starting transfers between devices, extended_2(): lax.ppermute(lax.slice_in_dim(block, block.shape[dim] - width, None, axis...  37.5 us
    ppermute x10, starting transfers between devices, from_behind(): return lax.ppermute(block, axis, route)  32.7 us
    ppermute x12, starting transfers between devices, extended_2(): lax.ppermute(lax.slice_in_dim(block, 0, width, axis=dim), axis, backward)  28.3 us
    concatenate x2, local copies, waits for them, and re-layouts, dense_conv(): jnp.concatenate(tap_list, axis=-1)  20.2 us
    ppermute x10, waiting for transfers between devices, from_behind(): return lax.ppermute(block, axis, route)  18.1 us
    ppermute x12, waiting for transfers between devices, extended_2(): lax.ppermute(lax.slice_in_dim(block, block.shape[dim] - width, None, axis...  12.4 us
    dot_general x2, matrix products, dense_conv(): jnp.dot(stacked, kernel.reshape(-1, channels), preferred_element_type=jnp...  9.19 us
    slice x6, local copies, waits for them, and re-layouts, dense_conv(): extended[step_t:step_t + frame_count, step_h:step_h + row_count, step_w:s...  8.32 us
  transfers between devices with their start and end apart: 35, of which 15 were waited for; matrix products, arithmetic and copies ran while one was open for 28% of the time, Pallas kernels for 0%

commit v1 on v0

--- a/solution.py
+++ b/solution.py
@@ -1,7 +1,551 @@
+import functools
+
 import jax
 import jax.numpy as jnp
 from jax import lax
+from jax.experimental import pallas as pl
+from jax.experimental.pallas import tpu as pltpu
 from jax.sharding import PartitionSpec as P
+
+FRAME_REACH = 2
+TEACHER_HALO = 2
+VMEM_BYTES = 56 * 1024 * 1024
+
+
+def student_halos(layers):
+    halos = [0] * (layers + 1)
+    for layer in reversed(range(layers)):
+        halos[layer] = max(layer, halos[layer + 1] + 1)
+    return halos
+
+
+def slot_of(source, own, slots):
+    difference = source ^ own
+    bits = slots.bit_length() - 1
+    slot = 0
+    for bit in range(bits):
+        slot = slot | (((difference >> bit) & 1) << (bits - 1 - bit))
+    return slot
+
+
+def row_position(rows_each):
+    time = lax.axis_index("ta")
+    chain = lax.axis_index("ha") * lax.axis_size("wa") + lax.axis_index("wa")
+    count = lax.axis_size("ta")
+    part = time ^ ((chain & 1) * (count - 1))
+    return time, chain, part, (chain * count + part) * rows_each
+
+
+def row_mask(row, total):
+    return jnp.where((row >= 0) & (row < total), 1.0, 0.0).astype(jnp.float32)
+
+
+def moved(field, step):
+    width = field.shape[-2]
+    rolled = pltpu.roll(field, step % width, field.ndim - 2)
+    column = lax.broadcasted_iota(jnp.int32, field.shape, field.ndim - 2)
+    lost = 0 if step > 0 else width - 1
+    return jnp.where(column == lost, 0.0, rolled)
+
+
+def tap_sum(read, taps, flip):
+    sides = [None, None, None]
+    for step_t in range(3):
+        for step_h in range(3):
+            block = read(step_t, step_h)
+            for step_w in range(3):
+                tap = (2 - step_t, 2 - step_h, 2 - step_w) if flip else (step_t, step_h, step_w)
+                term = block * taps[tap]
+                sides[step_w] = term if sides[step_w] is None else sides[step_w] + term
+    return sides[1] + moved(sides[0], 1) + moved(sides[2], -1)
+
+
+def load_taps(depth_ref, layer):
+    taps = {}
+    for step_t in range(3):
+        for step_h in range(3):
+            for step_w in range(3):
+                line = (step_t * 3 + step_h) * 3 + step_w
+                taps[(step_t, step_h, step_w)] = depth_ref[layer, line : line + 1, :]
+    return taps
+
+
+def forward_kernel(rows_each, total_rows, halos, parts_ref, depth_ref, point_ref, *refs):
+    layers = len(halos) - 1
+    last_ref = refs[0]
+    slope_refs = refs[1 : 1 + layers]
+    state_ref, active_ref, mixed_ref = refs[1 + layers :]
+    slots, own_frames, _, width, channels = parts_ref.shape
+    frames = slots * own_frames
+    time, _, _, first_row = row_position(rows_each)
+
+    def start(t, carry):
+        state_ref[t] = parts_ref[slot_of(t // own_frames, time, slots), t % own_frames].astype(
+            jnp.float32
+        )
+        return carry
+
+    lax.fori_loop(0, frames, start, 0)
+    active_ref[0:FRAME_REACH] = jnp.zeros((FRAME_REACH,) + active_ref.shape[1:], jnp.float32)
+    for layer in range(layers):
+        halo, out_halo = halos[layer], halos[layer + 1]
+        shift = halos[0] - halo
+        out_rows = rows_each + 2 * out_halo
+
+        def activate(t, carry, halo=halo, shift=shift, layer=layer):
+            for row in range(rows_each + 2 * halo):
+                value = state_ref[t, shift + row]
+                sigma = jax.nn.sigmoid(value)
+                active = (value * sigma).astype(jnp.bfloat16).astype(jnp.float32)
+                active_ref[t + FRAME_REACH, shift + row] = active * row_mask(
+                    first_row + row - halo, total_rows
+                )
+                slope_row = row - (halo - layer)
+                if 0 <= slope_row < rows_each + 2 * layer:
+                    slope_refs[layer][t, slope_row] = sigma * (1.0 + value * (1.0 - sigma))
+            return carry
+
+        lax.fori_loop(0, frames, activate, 0)
+
+        def mix(t, carry, shift=shift, out_rows=out_rows, layer=layer, out_halo=out_halo):
+            taps = load_taps(depth_ref, layer)
+            for row in range(out_rows):
+                spread = tap_sum(
+                    lambda i, j, row=row: active_ref[t + i, shift + row + j], taps, False
+                )
+                mixed_ref[row * width : (row + 1) * width] = spread.astype(jnp.bfloat16)
+            mixed = jnp.dot(
+                mixed_ref[0 : out_rows * width],
+                point_ref[layer],
+                preferred_element_type=jnp.float32,
+            ).reshape(out_rows, width, channels)
+            following = state_ref[t, shift + 1 : shift + 1 + out_rows] + mixed
+            if layer == layers - 1:
+                last_ref[t] = following.astype(jnp.bfloat16)
+            else:
+                state_ref[t, shift + 1 : shift + 1 + out_rows] = following
+            return carry
+
+        if halo - out_halo == 1:
+            lax.fori_loop(0, frames, mix, 0)
+        else:
+            inner = halo - out_halo - 1
+
+            def mix_inner(t, carry, base=shift + inner, out_rows=out_rows, layer=layer):
+                return mix(t, carry, shift=base, out_rows=out_rows, layer=layer)
+
+            lax.fori_loop(0, frames, mix_inner, 0)
+
+
+def student_forward(parts, depth_weights, point_weights, rows_each, total_rows):
+    layers = depth_weights.shape[0]
+    halos = student_halos(layers)
+    slots, own_frames, rows, width, channels = parts.shape
+    frames = slots * own_frames
+    shapes = [jax.ShapeDtypeStruct((frames, rows_each, width, channels), jnp.bfloat16)]
+    for layer in range(layers):
+        shapes.append(
+            jax.ShapeDtypeStruct((frames, rows_each + 2 * layer, width, channels), jnp.float32)
+        )
+    return pl.pallas_call(
+        functools.partial(forward_kernel, rows_each, total_rows, halos),
+        out_shape=shapes,
+        scratch_shapes=[
+            pltpu.VMEM((frames, rows, width, channels), jnp.float32),
+            pltpu.VMEM((frames + FRAME_REACH, rows, width, channels), jnp.float32),
+            pltpu.VMEM((rows * width, channels), jnp.bfloat16),
+        ],
+        compiler_params=pltpu.CompilerParams(vmem_limit_bytes=VMEM_BYTES),
+        name="student_forward",
+    )(parts, depth_weights.reshape(layers, -1, channels), point_weights)
+
+
+def teacher_kernel(
+    rows_each, total_rows, parts_ref, weights_ref, last_ref, project_ref, wide_ref, narrow_ref,
+    kernel_ref, active_ref, sum_ref, copy_sems,
+):
+    slots, own_frames, rows, width, channels = parts_ref.shape
+    frames = slots * own_frames
+    padded = kernel_ref.shape[3] // 3
+    time, _, _, first_row = row_position(rows_each)
+
+    def copies(conv):
+        return [
+            pltpu.make_async_copy(
+                weights_ref.at[conv, :, side],
+                kernel_ref.at[conv, :, 0, pl.ds(side * padded, channels), :],
+                copy_sems.at[conv, side],
+            )
+            for side in range(3)
+        ]
+
+    for conv in range(2):
+        for copy in copies(conv):
+            copy.start()
+    for conv in range(2):
+        for side in range(3):
+            kernel_ref[conv, :, 0, side * padded + channels : (side + 1) * padded, :] = jnp.zeros(
+                (9, padded - channels, channels), jnp.bfloat16
+            )
+
+    active_ref[...] = jnp.zeros(active_ref.shape, jnp.bfloat16)
+
+    def source(t):
+        return slot_of(t // own_frames, time, slots), t % own_frames
+
+    def spread_columns(t, row, value):
+        for side in range(3):
+            piece = value if side == 1 else moved(value, 1 - side)
+            active_ref[t + FRAME_REACH, row, :, side * padded : side * padded + channels] = (
+                piece.astype(jnp.bfloat16)
+            )
+
+    def activated(value):
+        mean = jnp.mean(value * value, axis=-1, keepdims=True)
+        normed = value * lax.rsqrt(mean + 1e-06)
+        return (normed * jax.nn.sigmoid(normed)).astype(jnp.bfloat16).astype(jnp.float32)
+
+    def first(t, carry):
+        slot, frame = source(t)
+        for row in range(rows):
+            spread_columns(t, row, activated(parts_ref[slot, frame, row].astype(jnp.float32)))
+        return carry
+
+    lax.fori_loop(0, frames, first, 0)
+
+    def convolve(conv, out_rows):
+        def tap(index, carry):
+            step_t, step_h = index // 3, index % 3
+            field = active_ref[pl.ds(step_t, frames), pl.ds(step_h, out_rows)]
+            term = jnp.dot(
+                field.reshape(frames * out_rows * width, 3 * padded),
+                kernel_ref[conv, index, 0],
+                preferred_element_type=jnp.float32,
+            )
+
+            @pl.when(index == 0)
+            def _():
+                sum_ref[0 : frames * out_rows * width] = term
+
+            @pl.when(index > 0)
+            def _():
+                sum_ref[0 : frames * out_rows * width] += term
+
+            return carry
+
+        for copy in copies(conv):
+            copy.wait()
+        lax.fori_loop(0, 9, tap, 0)
+
+    convolve(0, rows - 2)
+
+    def second(t, carry):
+        for row in range(rows - 2):
+            base = (t * (rows - 2) + row) * width
+            value = sum_ref[pl.ds(pl.multiple_of(base, width), width), :]
+            spread_columns(
+                t, row, activated(value) * row_mask(first_row + row - 1, total_rows)
+            )
+        return carry
+
+    lax.fori_loop(0, frames, second, 0)
+    convolve(1, rows - 4)
+
+    def finish(t, carry):
+        slot, frame = source(t)
+        count = rows_each * width
+        summed = sum_ref[pl.ds(pl.multiple_of(t * count, count), count), :]
+        field = parts_ref[slot, frame, 2 : 2 + rows_each].astype(jnp.float32)
+        target = (field.reshape(count, channels) + summed).astype(jnp.bfloat16)
+        projected = jnp.dot(
+            last_ref[t].reshape(count, -1), project_ref[...], preferred_element_type=jnp.float32
+        )
+        mismatch = (projected - target.astype(jnp.float32)).astype(jnp.bfloat16)
+        gradient = lax.dot_general(
+            mismatch, project_ref[...], (((1,), (1,)), ((), ())),
+            preferred_element_type=jnp.float32,
+        ).reshape(rows_each, width, -1)
+        wide_ref[t] = gradient
+        narrow_ref[t] = gradient.astype(jnp.bfloat16)
+        return carry
+
+    lax.fori_loop(0, frames, finish, 0)
+
+
+def teacher_gradient(parts, weights, last, project_weight, rows_each, total_rows):
+    slots, own_frames, rows, width, channels = parts.shape
+    frames = slots * own_frames
+    padded = -(-channels // 128) * 128
+    student = last.shape[-1]
+    whole = pl.BlockSpec(memory_space=pltpu.VMEM)
+    shape = (frames, rows_each, width, student)
+    return pl.pallas_call(
+        functools.partial(teacher_kernel, rows_each, total_rows),
+        out_shape=[
+            jax.ShapeDtypeStruct(shape, jnp.float32),
+            jax.ShapeDtypeStruct(shape, jnp.bfloat16),
+        ],
+        in_specs=[whole, pl.BlockSpec(memory_space=pl.ANY), whole, whole],
+        scratch_shapes=[
+            pltpu.VMEM((2, 9, 1, 3 * padded, channels), jnp.bfloat16),
+            pltpu.VMEM((frames + FRAME_REACH, rows, width, 3 * padded), jnp.bfloat16),
+            pltpu.VMEM((frames * (rows - 2) * width, channels), jnp.float32),
+            pltpu.SemaphoreType.DMA((2, 3)),
+        ],
+        compiler_params=pltpu.CompilerParams(vmem_limit_bytes=VMEM_BYTES),
+        name="teacher_gradient",
+    )(parts, weights.reshape(2, 9, 3, channels, channels), last, project_weight)
+
+
+def backward_kernel(
+    rows_each, total_rows, layers, wide_ref, low_ref, high_ref, depth_ref, point_ref, *refs
+):
+    slope_refs = refs[:layers]
+    out_ref, grad_ref, back_ref = refs[layers:]
+    frames, _, width, channels = wide_ref.shape
+    _, _, _, first_row = row_position(rows_each)
+    grad_ref[:, 0:layers] = low_ref[...].astype(jnp.float32)
+    grad_ref[:, layers : layers + rows_each] = wide_ref[...]
+    grad_ref[:, layers + rows_each :] = high_ref[...].astype(jnp.float32)
+    back_ref[frames:] = jnp.zeros((FRAME_REACH,) + back_ref.shape[1:], jnp.float32)
+    for layer in reversed(range(layers)):
+        shift = layers - (layer + 1)
+        count = rows_each + 2 * (layer + 1)
+
+        def unmix(t, carry, shift=shift, count=count, layer=layer):
+            gradient = grad_ref[t, shift : shift + count].astype(jnp.bfloat16)
+            backward = lax.dot_general(
+                gradient.reshape(count * width, channels),
+                point_ref[layer],
+                (((1,), (1,)), ((), ())),
+                preferred_element_type=jnp.float32,
+            ).astype(jnp.bfloat16).astype(jnp.float32).reshape(count, width, channels)
+            for row in range(count):
+                back_ref[t, shift + row] = backward[row] * row_mask(
+                    first_row + row - (layer + 1), total_rows
+                )
+            return carry
+
+        lax.fori_loop(0, frames, unmix, 0)
+
+        def step(t, carry, shift=shift, count=count, layer=layer):
+            taps = load_taps(depth_ref, layer)
+            for row in range(count - 2):
+                spread = tap_sum(
+                    lambda i, j, row=row: back_ref[t + i, shift + row + j], taps, True
+                )
+                value = grad_ref[t, shift + 1 + row] + spread * slope_refs[layer][t, row]
+                if layer == 0:
+                    out_ref[t, row] = value.astype(jnp.bfloat16)
+                else:
+                    grad_ref[t, shift + 1 + row] = value
+            return carry
+
+        lax.fori_loop(0, frames, step, 0)
+
+
+def student_backward(
+    wide, low, high, depth_weights, point_weights, slopes, rows_each, total_rows
+):
+    layers = depth_weights.shape[0]
+    frames, _, width, channels = wide.shape
+    rows = rows_each + 2 * layers
+    return pl.pallas_call(
+        functools.partial(backward_kernel, rows_each, total_rows, layers),
+        out_shape=jax.ShapeDtypeStruct(wide.shape, jnp.bfloat16),
+        scratch_shapes=[
+            pltpu.VMEM((frames, rows, width, channels), jnp.float32),
+            pltpu.VMEM((frames + FRAME_REACH, rows, width, channels), jnp.float32),
+        ],
+        compiler_params=pltpu.CompilerParams(vmem_limit_bytes=VMEM_BYTES),
+        name="student_backward",
+    )(wide, low, high, depth_weights.reshape(layers, -1, channels), point_weights, *slopes)
+
+
+AXES = ("ta", "ha", "wa")
+
+
+def whole_route(sizes, move):
+    times, heights, widths = sizes
+    route = []
+    for time in range(times):
+        for height in range(heights):
+            for side in range(widths):
+                target = move(time, height, side)
+                if target is None:
+                    continue
+                goal, up, across = target
+                if 0 <= up < heights:
+                    route.append(
+                        (
+                            (time * heights + height) * widths + side,
+                            (goal * heights + up) * widths + across,
+                        )
+                    )
+    return route
+
+
+def chain_swap(parity, widths, longest):
+    def move(time, height, side):
+        chain = height * widths + side
+        other = chain + 1 if chain % 2 == parity else chain - 1
+        if not 0 <= other < longest:
+            return None
+        return time, other // widths, other % widths
+
+    return move
+
+
+def rows_of(block, begin, count, axis):
+    return lax.dynamic_slice_in_dim(block, begin, count, axis=axis)
+
+
+def over_time(block, halo, rows_each):
+    time, _, part, _ = row_position(rows_each)
+    count = lax.axis_size("ta")
+    parts = block[None]
+    distance = count // 2
+    while distance:
+        rows = rows_each * distance + 2 * halo
+        upper = (part // distance) % 2
+        kept = rows_of(parts, upper * rows_each * distance, rows, 2)
+        sent = rows_of(parts, (1 - upper) * rows_each * distance, rows, 2)
+        got = lax.ppermute(sent, "ta", [(i, i ^ distance) for i in range(count)])
+        parts = jnp.concatenate([kept, got], axis=0)
+        distance //= 2
+    return parts
+
+
+def gather_student(block, halo, rows_each, sizes):
+    _, chain, _, _ = row_position(rows_each)
+    rows = block.shape[1]
+    longest = sizes[1] * sizes[2]
+    even = chain % 2 == 0
+    start = jnp.where(even, rows - halo, 0)
+    swap_even = lax.ppermute(
+        rows_of(block, start, halo, 1), AXES, whole_route(sizes, chain_swap(0, sizes[2], longest))
+    )
+    swap_odd = lax.ppermute(
+        rows_of(block, rows - halo - start, halo, 1),
+        AXES,
+        whole_route(sizes, chain_swap(1, sizes[2], longest)),
+    )
+    low = jnp.where(even, swap_odd, swap_even)
+    high = jnp.where(even, swap_even, swap_odd)
+    return over_time(jnp.concatenate([low, block, high], axis=1), halo, rows_each)
+
+
+def gather_teacher(tile, halo, rows_each, sizes):
+    side = lax.axis_index("wa")
+    rows = tile.shape[1] // 2
+    left = side == 0
+
+    def for_side(which):
+        block = rows_of(tile, which * (rows - halo), rows + halo, 1)
+        edge = rows_of(tile, (1 - which) * (2 * rows - halo), halo, 1)
+        return jnp.concatenate([block, edge], axis=1)
+
+    mine = for_side(side)
+    other = lax.ppermute(for_side(1 - side), "wa", [(0, 1), (1, 0)])
+    full = jnp.concatenate(
+        [jnp.where(left, mine, other), jnp.where(left, other, mine)], axis=2
+    )
+    block, edge = full[:, : rows + halo], full[:, rows + halo :]
+    beyond = lax.ppermute(
+        edge,
+        AXES,
+        whole_route(sizes, lambda time, up, across: (time, up + (1 - 2 * across), across)),
+    )
+    extended = jnp.where(
+        left,
+        jnp.concatenate([beyond, block], axis=1),
+        jnp.concatenate([block, beyond], axis=1),
+    )
+    return over_time(extended, halo, rows_each)
+
+
+def gradient_borders(narrow, halo, rows_each, sizes):
+    times, heights, widths = sizes
+    _, _, part, _ = row_position(rows_each)
+    longest = heights * widths
+    even = part % 2 == 0
+
+    def place(time, height, side):
+        chain = height * widths + side
+        return chain * times + (time ^ ((chain & 1) * (times - 1)))
+
+    def swap(parity):
+        def move(time, height, side):
+            position = place(time, height, side)
+            other = position + 1 if position % 2 == parity else position - 1
+            if not 0 <= other < longest * times:
+                return None
+            chain, index = divmod(other, times)
+            return index ^ ((chain & 1) * (times - 1)), chain // widths, chain % widths
+
+        return whole_route(sizes, move)
+
+    top = narrow[:, narrow.shape[1] - halo :]
+    bottom = narrow[:, :halo]
+    outer = lax.ppermute(jnp.where(even, bottom, top), AXES, swap(1))
+    inner = lax.ppermute(jnp.where(even, top, bottom), AXES, swap(0))
+    return jnp.where(even, outer, inner), jnp.where(even, inner, outer)
+
+
+def give_back(out, rows_each):
+    time, _, part, _ = row_position(rows_each)
+    count = lax.axis_size("ta")
+    frames = out.shape[0] // count
+    pieces = []
+    for difference in range(count):
+        sent = rows_of(out, (time ^ difference) * frames, frames, 0)
+        if difference:
+            sent = lax.ppermute(sent, "ta", [(i, i ^ difference) for i in range(count)])
+        pieces.append(sent)
+    stacked = jnp.stack(pieces)
+    ordered = [
+        lax.dynamic_index_in_dim(stacked, part ^ index, 0, keepdims=False)
+        for index in range(count)
+    ]
+    return jnp.concatenate(ordered, axis=1)
+
+
+def gathered(sizes, total_rows):
+    rows_each = total_rows // (sizes[0] * sizes[1] * sizes[2])
+
+    def on_device_gathered(
+        teacher_in, teacher_weights, student_in, depth_weights, point_weights, project_weight
+    ):
+        layers = depth_weights.shape[0]
+        halo = student_halos(layers)[0]
+        student_parts = gather_student(student_in, halo, rows_each, sizes)
+        teacher_parts = gather_teacher(teacher_in, TEACHER_HALO, rows_each, sizes)
+        last, *slopes = student_forward(
+            student_parts, depth_weights, point_weights, rows_each, total_rows
+        )
+        wide, narrow = teacher_gradient(
+            teacher_parts, teacher_weights[0], last, project_weight, rows_each, total_rows
+        )
+        low, high = gradient_borders(narrow, layers, rows_each, sizes)
+        out = student_backward(
+            wide, low, high, depth_weights, point_weights, slopes, rows_each, total_rows
+        )
+        return give_back(out, rows_each)
+
+    return on_device_gathered
+
+
+def can_gather(sizes, shape_rows, width, layers):
+    times, heights, widths = sizes
+    block = shape_rows // (heights * widths)
+    return (
+        widths == 2
+        and times & (times - 1) == 0
+        and block % times == 0
+        and block // times >= max(layers, TEACHER_HALO)
+        and block >= student_halos(layers)[0]
+        and width % 16 == 0
+    )
 
 
 def from_behind(block, axis, distance):
@@ -156,11 +700,22 @@
 
 
 def solution(mesh):
+    sizes = tuple(mesh.shape[axis] for axis in AXES)
     placed = (P("ta", "ha", "wa", None), P(), P("ta", ("ha", "wa"), None, None), P(), P(), P())
-    return jax.shard_map(
-        on_device,
-        mesh=mesh,
-        in_specs=placed,
-        out_specs=P("ta", ("ha", "wa"), None, None),
-        check_vma=False,
-    )
+
+    def whole(
+        teacher_in, teacher_weights, student_in, depth_weights, point_weights, project_weight
+    ):
+        total_rows, width = student_in.shape[1], student_in.shape[2]
+        body = on_device
+        if can_gather(sizes, total_rows, width, depth_weights.shape[0]):
+            body = gathered(sizes, total_rows)
+        return jax.shard_map(
+            body,
+            mesh=mesh,
+            in_specs=placed,
+            out_specs=P("ta", ("ha", "wa"), None, None),
+            check_vma=False,
+        )(teacher_in, teacher_weights, student_in, depth_weights, point_weights, project_weight)
+
+    return whole

time: 212 us -> 83.7 us (0.39); the launches traced: 209 us -> 83.3 us
  starting transfers between devices: 102 us -> 23.2 us
  Pallas kernels: 0 us -> 40.3 us
  local copies, waits for them, and re-layouts: 39.7 us -> 4.88 us
  waiting for transfers between devices: 33.8 us -> 10.2 us
  matrix products: 16.1 us -> 0 us
  other arithmetic: 13.6 us -> 4.47 us
  between operations: 3.33 us -> 0.17 us
    ppermute x34 -> x13, starting transfers between devices: 98.6 us -> 23.2 us  [the longest x4 10.3 us: over_time(): got = lax.ppermute(sent, 'ta', [(i, i ^ distance) for i in range(count)])]
    pallas_call x0 -> x3, Pallas kernels: none -> 40.3 us  [the longest x1 15.6 us: teacher_gradient(): pl.pallas_call(functools.partial(teacher_kernel, rows_each, total_rows),...]
    ppermute x34 -> x13, waiting for transfers between devices: 30.5 us -> 10.2 us  [the longest x1 3.65 us: gradient_borders(): outer = lax.ppermute(jnp.where(even, bottom, top), AXES, swap(1))]
    concatenate x2 -> x0, local copies, waits for them, and re-layouts: 20.2 us -> none  [dense_conv(): jnp.concatenate(tap_list, axis=-1)]
    dot_general x11 -> x0, matrix products: 16.1 us -> none  [the longest x2 9.19 us: dense_conv(): jnp.dot(stacked, kernel.reshape(-1, channels), preferred_element_type=jnp...]
    slice x8 -> x0, local copies, waits for them, and re-layouts: 14 us -> none  [the longest x6 8.32 us: dense_conv(): extended[step_t:step_t + frame_count, step_h:step_h + row_count, step_w:s...]
    convert_element_type x7 -> x0, other arithmetic: 6.39 us -> none  [the longest x3 2.5 us: student_pass(): gradient.astype(jnp.bfloat16).reshape(-1, channels)]
    mul x8 -> x0, local copies, waits for them, and re-layouts: 3.73 us -> none  [depthwise(): tap_slice.astype(jnp.float32) * kernel[step_t, step_h, step_w]]
  transfers between devices with their start and end apart: 35 -> 13, of which waited for: 15 -> 5; matrix products, arithmetic and copies ran while one was open for 28% -> 6% of each run, Pallas kernels for 0% -> 16%
where the time goes in v1:
time: 83.7 us; the launch traced here: 83.3 us
  Pallas kernels  40.3 us (48%)
  starting transfers between devices  23.2 us (28%)
  waiting for transfers between devices  10.2 us (12%)
  local copies, waits for them, and re-layouts  4.88 us (6%)
  other arithmetic  4.47 us (5%)
    pallas_call x1, Pallas kernels, teacher_gradient(): pl.pallas_call(functools.partial(teacher_kernel, rows_each, total_rows),...  15.6 us
    pallas_call x1, Pallas kernels, student_forward(): pl.pallas_call(functools.partial(forward_kernel, rows_each, total_rows, h...  13.3 us
    pallas_call x1, Pallas kernels, student_backward(): pl.pallas_call(functools.partial(backward_kernel, rows_each, total_rows,...  11.5 us
    ppermute x4, starting transfers between devices, over_time(): got = lax.ppermute(sent, 'ta', [(i, i ^ distance) for i in range(count)])  10.3 us
    ppermute x1, waiting for transfers between devices, gradient_borders(): outer = lax.ppermute(jnp.where(even, bottom, top), AXES, swap(1))  3.65 us
    ppermute x1, starting transfers between devices, gradient_borders(): outer = lax.ppermute(jnp.where(even, bottom, top), AXES, swap(1))  3.03 us
    ppermute x1, starting transfers between devices, gather_student(): lax.ppermute(rows_of(block, rows - halo - start, halo, 1), AXES, whole_ro...  3.02 us
    ppermute x3, starting transfers between devices, give_back(): sent = lax.ppermute(sent, 'ta', [(i, i ^ difference) for i in range(count)])  2.98 us
  transfers between devices with their start and end apart: 13, of which 5 were waited for; matrix products, arithmetic and copies ran while one was open for 6% of the time, Pallas kernels for 16%

profile of v1, /device:TPU:17, one launch (start us, length us, event | category | flops | bytes accessed | tf_op | source)
XLA Modules:
  0.0 83.3 jit_solution(7877967529209658390)
XLA Ops:
  0.0 0.8 %constant_dynamic-slice_fusion.4 = (bf16[2,6,16,128]{3,2,1,0:T(8,128)(2,1)S(1)}, bf16[2,6,16,128]{3,2,1,0:T(8,128)(2,1)S(1)}) fusion(bf16[2,16,16,128]{3,2,1,0:T(8,128)(2,1)} %param.8, s32[]{:T(128)S(6)} %select_n.164, s32[]{:T(128)S(6)} %select_n.163), kind=kLoop, calls=%fused_computation.41 | loop fusion | bytes 196616 | tf_op jit(solution)/shard_map/dynamic_slice | solution.py:400
  0.8 3.0 %collective-permute-start.4 = (bf16[2,6,16,128]{3,2,1,0:T(8,128)(2,1)S(1)}, bf16[2,6,16,128]{3,2,1,0:T(8,128)(2,1)S(1)}, u32[]{:S(2)}, u32[]{:S(2)}) collective-permute-start(bf16[2,6,16,128]{3,2,1,0:T(8,128)(2,1)S(1)} %get-tuple-element.43), channel_id=1, source_target_pairs={{1,2},{2,1},{3,4},{4,3},{5,6},{6,5},{9,10},{10,9},{11,12},{12,11},... | collective-permute-start | bytes 147464 | tf_op jit(solution)/shard_map/ppermute | solution.py:428
  3.9 1.4 %collective-permute-start.5 = (bf16[2,6,16,128]{3,2,1,0:T(8,128)(2,1)S(1)}, bf16[2,6,16,128]{3,2,1,0:T(8,128)(2,1)S(1)}, u32[]{:S(2)}, u32[]{:S(2)}) collective-permute-start(bf16[2,6,16,128]{3,2,1,0:T(8,128)(2,1)S(1)} %get-tuple-element.44), channel_id=1, source_target_pairs={{0,1},{1,0},{2,3},{3,2},{4,5},{5,4},{6,7},{7,6},{8,9},{9,8},{10,11... | collective-permute-start | bytes 147464 | tf_op jit(solution)/shard_map/ppermute | solution.py:425
  5.3 1.0 %constant_dynamic-slice_fusion.8 = (bf16[2,18,8,192]{3,2,1,0:T(8,128)(2,1)S(1)}, bf16[2,18,8,192]{3,2,1,0:T(8,128)(2,1)S(1)}) fusion(bf16[2,32,8,192]{3,2,1,0:T(8,128)(2,1)} %param.6, s32[]{:T(128)S(6)} %select_n.147, s32[]{:T(128)S(6)} %select_n.149), kind=kLoop, calls=%fused_computation.45 | loop fusion | bytes 442376 | tf_op jit(solution)/shard_map/dynamic_slice | solution.py:400
  6.3 0.8 constant_dynamic-slice_fusion.7
  7.1 0.2 collective-permute-start
  7.3 0.9 %pad_maximum_fusion.3 = bf16[2,28,16,128]{3,2,1,0:T(8,128)(2,1)S(1)} fusion(bf16[2,6,16,128]{3,2,1,0:T(8,128)(2,1)S(1)} %get-tuple-element.46, bf16[2,16,16,128]{3,2,1,0:T(8,128)(2,1)} %param.8, bf16[2,6,16,128]{3,2,1,0:T(8,128)(2,1)S(1)} %get-tuple-element.45), kind=kLoop, calls=%fused_computation.16 | loop fusion | flops 229376 | bytes 458752 | tf_op jit(solution)/shard_map/concatenate | solution.py:435
  8.3 1.3 %collective-permute-start.6 = (bf16[1,2,20,16,128]{4,3,2,1,0:T(8,128)(2,1)S(1)}, bf16[1,2,20,16,128]{4,3,2,1,0:T(8,128)(2,1)S(1)}, u32[]{:S(2)}, u32[]{:S(2)}) collective-permute-start(bf16[1,2,20,16,128]{4,3,2,1,0:T(8,128)(2,1)S(1)} %get-tuple-element.33), channel_id=1, source_target_pairs={{0,16},{8,24},{16,0},{24,8},{1,17},{9,25},{17,1},{25,9},{2,18},{10... | collective-permute-start | bytes 491528 | tf_op jit(solution)/shard_map/ppermute | solution.py:413
  9.6 2.1 %collective-permute-done = bf16[2,20,8,192]{3,2,1,0:T(8,128)(2,1)S(1)} collective-permute-done((bf16[2,20,8,192]{3,2,1,0:T(8,128)(2,1)S(1)}, bf16[2,20,8,192]{3,2,1,0:T(8,128)(2,1)S(1)}, u32[]{:S(2)}, u32[]{:S(2)}) %collective-permute-start) | collective-permute-done | bytes 122912 | tf_op jit(solution)/shard_map/ppermute | solution.py:449
  11.7 2.3 %collective-permute-start.1 = (bf16[2,2,16,192]{3,2,1,0:T(8,128)(2,1)S(1)}, bf16[2,2,16,192]{3,2,1,0:T(8,128)(2,1)S(1)}, u32[]{:S(2)}, u32[]{:S(2)}) collective-permute-start(bf16[2,2,16,192]{3,2,1,0:T(8,128)(2,1)S(1)} %pad_maximum_fusion.8), channel_id=1, source_target_pairs={{0,2},{2,4},{3,1},{4,6},{5,3},{7,5},{8,10},{10,12},{11,9},{12,14},... | collective-permute-start | bytes 73736 | tf_op jit(solution)/shard_map/ppermute | solution.py:454
  14.1 2.3 %collective-permute-done.1 = bf16[2,2,16,192]{3,2,1,0:T(8,128)(2,1)S(1)} collective-permute-done((bf16[2,2,16,192]{3,2,1,0:T(8,128)(2,1)S(1)}, bf16[2,2,16,192]{3,2,1,0:T(8,128)(2,1)S(1)}, u32[]{:S(2)}, u32[]{:S(2)}) %collective-permute-start.1) | collective-permute-done | bytes 24608 | tf_op jit(solution)/shard_map/ppermute | solution.py:454
  16.4 0.1 maximum_select_fusion
  16.6 1.3 %collective-permute-start.2 = (bf16[1,2,12,16,192]{4,3,2,1,0:T(8,128)(2,1)S(1)}, bf16[1,2,12,16,192]{4,3,2,1,0:T(8,128)(2,1)S(1)}, u32[]{:S(2)}, u32[]{:S(2)}) collective-permute-start(bf16[1,2,12,16,192]{4,3,2,1,0:T(8,128)(2,1)S(1)} %get-tuple-element.23), channel_id=1, source_target_pairs={{0,16},{8,24},{16,0},{24,8},{1,17},{9,25},{17,1},{25,9},{2,18},{10... | collective-permute-start | bytes 442376 | tf_op jit(solution)/shard_map/ppermute | solution.py:413
  17.9 3.6 %collective-permute-start.7 = (bf16[2,2,16,16,128]{4,3,2,1,0:T(8,128)(2,1)S(1)}, bf16[2,2,16,16,128]{4,3,2,1,0:T(8,128)(2,1)S(1)}, u32[]{:S(2)}, u32[]{:S(2)}) collective-permute-start(bf16[2,2,16,16,128]{4,3,2,1,0:T(8,128)(2,1)S(1)} %get-tuple-element.22), channel_id=1, source_target_pairs={{0,8},{8,0},{16,24},{24,16},{1,9},{9,1},{17,25},{25,17},{2,10},{10... | collective-permute-start | bytes 786440 | tf_op jit(solution)/shard_map/ppermute | solution.py:413
  21.5 0.1 fusion.3
  21.6 4.1 %collective-permute-start.3 = (bf16[2,2,8,16,192]{4,3,2,1,0:T(8,128)(2,1)S(1)}, bf16[2,2,8,16,192]{4,3,2,1,0:T(8,128)(2,1)S(1)}, u32[]{:S(2)}, u32[]{:S(2)}) collective-permute-start(bf16[2,2,8,16,192]{4,3,2,1,0:T(8,128)(2,1)S(1)} %get-tuple-element.20), channel_id=1, source_target_pairs={{0,8},{8,0},{16,24},{24,16},{1,9},{9,1},{17,25},{25,17},{2,10},{10... | collective-permute-start | bytes 589832 | tf_op jit(solution)/shard_map/ppermute | solution.py:413
  25.7 0.6 copy.9.depth_ref
  26.4 0.7 copy.10.project_ref
  27.1 0.8 pad_maximum_fusion.1.parts_ref
  27.9 13.3 %student_forward.1 = (bf16[8,4,16,128]{3,2,1,0:T(8,128)(2,1)}, f32[8,4,16,128]{3,2,1,0:T(8,128)}, f32[8,6,16,128]{3,2,1,0:T(8,128)}, f32[8,8,16,128]{3,2,1,0:T(8,128)}, f32[8,10,16,128]{3,2,1,0:T(8,128)}) custom-call(bf16[4,2,16,16,128]{4,3,2,1,0:T(8,128)(2,1)} %pad_maximum_fusion.1.parts_ref, f32[4,27,128]{2,1,0:T(8,128)} %copy.9.depth_ref, ...), custom_call_target="tpu_custom_call" | custom-call | tf_op jit(solution)/shard_map/student_forward/pallas_call | solution.py:150
  41.2 0.9 %pad_maximum_fusion.parts_ref = bf16[4,2,8,16,192]{4,3,2,1,0:T(8,128)(2,1)} fusion(bf16[2,2,8,16,192]{4,3,2,1,0:T(8,128)(2,1)S(1)} %collective-permute-done.3, bf16[2,2,8,16,192]{4,3,2,1,0:T(8,128)(2,1)S(1)} %get-tuple-element.19), kind=kLoop, calls=%fused_computation | loop fusion | flops 196608 | bytes 786432 | tf_op jit(solution)/shard_map/concatenate | solution.py:414
  42.1 15.6 %teacher_gradient.1 = (f32[8,4,16,128]{3,2,1,0:T(8,128)}, bf16[8,4,16,128]{3,2,1,0:T(8,128)(2,1)}) custom-call(bf16[4,2,8,16,192]{4,3,2,1,0:T(8,128)(2,1)} %pad_maximum_fusion.parts_ref, bf16[2,9,3,192,192]{4,3,2,1,0:T(8,128)(2,1)} %bitcast.23, bf16[8,4,16,128]{3,2,1,0:T(8,128)(2,1)} %get-tuple-element.12.last_ref, bf16[128,192]{1,0:T(8,128)(2,1)} %copy.10.project_ref), custom_call_target="tpu_custom_call" | custom-call | tf_op jit(solution)/shard_map/teacher_gradient/pallas_call | solution.py:282
  57.7 3.0 %collective-permute-start.8 = (bf16[8,4,16,128]{3,2,1,0:T(8,128)(2,1)}, bf16[8,4,16,128]{3,2,1,0:T(8,128)(2,1)S(1)}, u32[]{:S(2)}, u32[]{:S(2)}) collective-permute-start(bf16[8,4,16,128]{3,2,1,0:T(8,128)(2,1)} %get-tuple-element.14), channel_id=1, source_target_pairs={{1,2},{2,1},{3,4},{4,3},{5,6},{6,5},{8,16},{9,17},{10,18},{11,19},... | collective-permute-start | bytes 393224 | tf_op jit(solution)/shard_map/ppermute | solution.py:490
  60.8 3.7 %collective-permute-done.8 = bf16[8,4,16,128]{3,2,1,0:T(8,128)(2,1)S(1)} collective-permute-done((bf16[8,4,16,128]{3,2,1,0:T(8,128)(2,1)}, bf16[8,4,16,128]{3,2,1,0:T(8,128)(2,1)S(1)}, u32[]{:S(2)}, u32[]{:S(2)}) %collective-permute-start.8) | collective-permute-done | bytes 131104 | tf_op jit(solution)/shard_map/ppermute | solution.py:490
  64.5 0.7 broadcast_select_fusion.2
  65.2 11.5 %student_backward.1 = bf16[8,4,16,128]{3,2,1,0:T(8,128)(2,1)} custom-call(f32[8,4,16,128]{3,2,1,0:T(8,128)} %get-tuple-element.13.wide_ref, bf16[8,4,16,128]{3,2,1,0:T(8,128)(2,1)} %get-tuple-element.28.low_ref, bf16[8,4,16,128]{3,2,1,0:T(8,128)(2,1)} %get-tuple-element.27.high_ref, f32[4,27,128]{2,1,0:T(8,128)} %copy.9.depth_ref, ...), custom_call_target="tpu_custom_call" | custom-call | tf_op jit(solution)/shard_map/student_backward/pallas_call | solution.py:353
  76.6 0.8 dynamic-slice_bitcast_fusion.8
  77.4 1.3 %collective-permute-start.10 = (bf16[2,4,16,128]{3,2,1,0:T(8,128)(2,1)S(1)}, bf16[2,4,16,128]{3,2,1,0:T(8,128)(2,1)S(1)}, u32[]{:S(2)}, u32[]{:S(2)}) collective-permute-start(bf16[2,4,16,128]{3,2,1,0:T(8,128)(2,1)S(1)} %get-tuple-element.42), channel_id=1, source_target_pairs={{0,8},{8,0},{16,24},{24,16},{1,9},{9,1},{17,25},{25,17},{2,10},{10... | collective-permute-start | bytes 98312 | tf_op jit(solution)/shard_map/ppermute | solution.py:503
  78.7 1.7 %collective-permute-start.12 = (bf16[2,4,16,128]{3,2,1,0:T(8,128)(2,1)S(1)}, bf16[2,4,16,128]{3,2,1,0:T(8,128)(2,1)S(1)}, u32[]{:S(2)}, u32[]{:S(2)}) collective-permute-start(bf16[2,4,16,128]{3,2,1,0:T(8,128)(2,1)S(1)} %get-tuple-element.40), channel_id=1, source_target_pairs={{0,24},{8,16},{16,8},{24,0},{1,25},{9,17},{17,9},{25,1},{2,26},{10... | collective-permute-start | bytes 98312 | tf_op jit(solution)/shard_map/ppermute | solution.py:503
  80.4 1.1 %collective-permute-done.11 = bf16[2,4,16,128]{3,2,1,0:T(8,128)(2,1)S(1)} collective-permute-done((bf16[2,4,16,128]{3,2,1,0:T(8,128)(2,1)S(1)}, bf16[2,4,16,128]{3,2,1,0:T(8,128)(2,1)S(1)}, u32[]{:S(2)}, u32[]{:S(2)}) %collective-permute-start.11) | collective-permute-done | bytes 32800 | tf_op jit(solution)/shard_map/ppermute | solution.py:503
  81.5 1.1 %collective-permute-done.12 = bf16[2,4,16,128]{3,2,1,0:T(8,128)(2,1)S(1)} collective-permute-done((bf16[2,4,16,128]{3,2,1,0:T(8,128)(2,1)S(1)}, bf16[2,4,16,128]{3,2,1,0:T(8,128)(2,1)S(1)}, u32[]{:S(2)}, u32[]{:S(2)}) %collective-permute-start.12) | collective-permute-done | bytes 32800 | tf_op jit(solution)/shard_map/ppermute | solution.py:503
  82.6 0.7 pad_maximum_fusion.7
  (24 shorter events, 0.4 us)
Async XLA Ops:
  0.0 25.7 %copy-start = (f32[4,3,3,3,128]{4,0,3,2,1:T(4,128)S(1)}, f32[4,3,3,3,128]{4,0,3,2,1:T(4,128)}, u32[]{:S(2)}) copy-start(f32[4,3,3,3,128]{4,0,3,2,1:T(4,128)} %param.9) | copy-start | bytes 165892
  0.0 26.4 %copy-start.1 = (bf16[128,192]{0,1:T(8,128)(2,1)S(1)}, bf16[128,192]{0,1:T(8,128)(2,1)}, u32[]{:S(2)}) copy-start(bf16[128,192]{0,1:T(8,128)(2,1)} %param.11) | copy-start | bytes 147460
  0.8 6.4 %collective-permute-start.4 = (bf16[2,6,16,128]{3,2,1,0:T(8,128)(2,1)S(1)}, bf16[2,6,16,128]{3,2,1,0:T(8,128)(2,1)S(1)}, u32[]{:S(2)}, u32[]{:S(2)}) collective-permute-start(bf16[2,6,16,128]{3,2,1,0:T(8,128)(2,1)S(1)} %get-tuple-element.43), channel_id=1, source_target_pairs={{1,2},{2,1},{3,4},{4,3},{5,6},{6,5},{9,10},{10,9},{11,12},{12,11},... | collective-permute-start | bytes 147464 | tf_op jit(solution)/shard_map/ppermute | solution.py:428
  3.9 3.4 %collective-permute-start.5 = (bf16[2,6,16,128]{3,2,1,0:T(8,128)(2,1)S(1)}, bf16[2,6,16,128]{3,2,1,0:T(8,128)(2,1)S(1)}, u32[]{:S(2)}, u32[]{:S(2)}) collective-permute-start(bf16[2,6,16,128]{3,2,1,0:T(8,128)(2,1)S(1)} %get-tuple-element.44), channel_id=1, source_target_pairs={{0,1},{1,0},{2,3},{3,2},{4,5},{5,4},{6,7},{7,6},{8,9},{9,8},{10,11... | collective-permute-start | bytes 147464 | tf_op jit(solution)/shard_map/ppermute | solution.py:425
  7.1 4.6 %collective-permute-start = (bf16[2,20,8,192]{3,2,1,0:T(8,128)(2,1)S(1)}, bf16[2,20,8,192]{3,2,1,0:T(8,128)(2,1)S(1)}, u32[]{:S(2)}, u32[]{:S(2)}) collective-permute-start(bf16[2,20,8,192]{3,2,1,0:T(8,128)(2,1)S(1)} %pad_maximum_fusion.5), channel_id=1, source_target_pairs={{0,1},{1,0},{2,3},{3,2},{4,5},{5,4},{6,7},{7,6},{8,9},{9,8},{10,11... | collective-permute-start | bytes 368648 | tf_op jit(solution)/shard_map/ppermute | solution.py:449
  8.3 9.6 %collective-permute-start.6 = (bf16[1,2,20,16,128]{4,3,2,1,0:T(8,128)(2,1)S(1)}, bf16[1,2,20,16,128]{4,3,2,1,0:T(8,128)(2,1)S(1)}, u32[]{:S(2)}, u32[]{:S(2)}) collective-permute-start(bf16[1,2,20,16,128]{4,3,2,1,0:T(8,128)(2,1)S(1)} %get-tuple-element.33), channel_id=1, source_target_pairs={{0,16},{8,24},{16,0},{24,8},{1,17},{9,25},{17,1},{25,9},{2,18},{10... | collective-permute-start | bytes 491528 | tf_op jit(solution)/shard_map/ppermute | solution.py:413
  11.7 4.7 %collective-permute-start.1 = (bf16[2,2,16,192]{3,2,1,0:T(8,128)(2,1)S(1)}, bf16[2,2,16,192]{3,2,1,0:T(8,128)(2,1)S(1)}, u32[]{:S(2)}, u32[]{:S(2)}) collective-permute-start(bf16[2,2,16,192]{3,2,1,0:T(8,128)(2,1)S(1)} %pad_maximum_fusion.8), channel_id=1, source_target_pairs={{0,2},{2,4},{3,1},{4,6},{5,3},{7,5},{8,10},{10,12},{11,9},{12,14},... | collective-permute-start | bytes 73736 | tf_op jit(solution)/shard_map/ppermute | solution.py:454
  16.6 4.9 %collective-permute-start.2 = (bf16[1,2,12,16,192]{4,3,2,1,0:T(8,128)(2,1)S(1)}, bf16[1,2,12,16,192]{4,3,2,1,0:T(8,128)(2,1)S(1)}, u32[]{:S(2)}, u32[]{:S(2)}) collective-permute-start(bf16[1,2,12,16,192]{4,3,2,1,0:T(8,128)(2,1)S(1)} %get-tuple-element.23), channel_id=1, source_target_pairs={{0,16},{8,24},{16,0},{24,8},{1,17},{9,25},{17,1},{25,9},{2,18},{10... | collective-permute-start | bytes 442376 | tf_op jit(solution)/shard_map/ppermute | solution.py:413
  17.9 9.2 %collective-permute-start.7 = (bf16[2,2,16,16,128]{4,3,2,1,0:T(8,128)(2,1)S(1)}, bf16[2,2,16,16,128]{4,3,2,1,0:T(8,128)(2,1)S(1)}, u32[]{:S(2)}, u32[]{:S(2)}) collective-permute-start(bf16[2,2,16,16,128]{4,3,2,1,0:T(8,128)(2,1)S(1)} %get-tuple-element.22), channel_id=1, source_target_pairs={{0,8},{8,0},{16,24},{24,16},{1,9},{9,1},{17,25},{25,17},{2,10},{10... | collective-permute-start | bytes 786440 | tf_op jit(solution)/shard_map/ppermute | solution.py:413
  21.6 19.6 %collective-permute-start.3 = (bf16[2,2,8,16,192]{4,3,2,1,0:T(8,128)(2,1)S(1)}, bf16[2,2,8,16,192]{4,3,2,1,0:T(8,128)(2,1)S(1)}, u32[]{:S(2)}, u32[]{:S(2)}) collective-permute-start(bf16[2,2,8,16,192]{4,3,2,1,0:T(8,128)(2,1)S(1)} %get-tuple-element.20), channel_id=1, source_target_pairs={{0,8},{8,0},{16,24},{24,16},{1,9},{9,1},{17,25},{25,17},{2,10},{10... | collective-permute-start | bytes 589832 | tf_op jit(solution)/shard_map/ppermute | solution.py:413
  57.7 6.8 %collective-permute-start.8 = (bf16[8,4,16,128]{3,2,1,0:T(8,128)(2,1)}, bf16[8,4,16,128]{3,2,1,0:T(8,128)(2,1)S(1)}, u32[]{:S(2)}, u32[]{:S(2)}) collective-permute-start(bf16[8,4,16,128]{3,2,1,0:T(8,128)(2,1)} %get-tuple-element.14), channel_id=1, source_target_pairs={{1,2},{2,1},{3,4},{4,3},{5,6},{6,5},{8,16},{9,17},{10,18},{11,19},... | collective-permute-start | bytes 393224 | tf_op jit(solution)/shard_map/ppermute | solution.py:490
  60.7 3.8 %collective-permute-start.9 = (bf16[8,4,16,128]{3,2,1,0:T(8,128)(2,1)}, bf16[8,4,16,128]{3,2,1,0:T(8,128)(2,1)S(1)}, u32[]{:S(2)}, u32[]{:S(2)}) collective-permute-start(bf16[8,4,16,128]{3,2,1,0:T(8,128)(2,1)} %get-tuple-element.14), channel_id=1, source_target_pairs={{0,8},{1,9},{2,10},{3,11},{4,12},{5,13},{6,14},{7,15},{8,0},{9,1},... | collective-permute-start | bytes 393224 | tf_op jit(solution)/shard_map/ppermute | solution.py:491
  77.4 3.0 %collective-permute-start.10 = (bf16[2,4,16,128]{3,2,1,0:T(8,128)(2,1)S(1)}, bf16[2,4,16,128]{3,2,1,0:T(8,128)(2,1)S(1)}, u32[]{:S(2)}, u32[]{:S(2)}) collective-permute-start(bf16[2,4,16,128]{3,2,1,0:T(8,128)(2,1)S(1)} %get-tuple-element.42), channel_id=1, source_target_pairs={{0,8},{8,0},{16,24},{24,16},{1,9},{9,1},{17,25},{25,17},{2,10},{10... | collective-permute-start | bytes 98312 | tf_op jit(solution)/shard_map/ppermute | solution.py:503
  78.7 2.8 %collective-permute-start.11 = (bf16[2,4,16,128]{3,2,1,0:T(8,128)(2,1)S(1)}, bf16[2,4,16,128]{3,2,1,0:T(8,128)(2,1)S(1)}, u32[]{:S(2)}, u32[]{:S(2)}) collective-permute-start(bf16[2,4,16,128]{3,2,1,0:T(8,128)(2,1)S(1)} %get-tuple-element.41), channel_id=1, source_target_pairs={{0,16},{8,24},{16,0},{24,8},{1,17},{9,25},{17,1},{25,9},{2,18},{10... | collective-permute-start | bytes 98312 | tf_op jit(solution)/shard_map/ppermute | solution.py:503
  78.7 3.8 %collective-permute-start.12 = (bf16[2,4,16,128]{3,2,1,0:T(8,128)(2,1)S(1)}, bf16[2,4,16,128]{3,2,1,0:T(8,128)(2,1)S(1)}, u32[]{:S(2)}, u32[]{:S(2)}) collective-permute-start(bf16[2,4,16,128]{3,2,1,0:T(8,128)(2,1)S(1)} %get-tuple-element.40), channel_id=1, source_target_pairs={{0,24},{8,16},{16,8},{24,0},{1,25},{9,17},{17,9},{25,1},{2,26},{10... | collective-permute-start | bytes 98312 | tf_op jit(solution)/shard_map/ppermute | solution.py:503
